TPU v7x, 128 devices: a whole 4x4x4 slice. The times are simulated.
128 devices in a mesh: row: 16 (over y, x), col: 4 (over z), depth: 2 (over core).
Axes of the slice: x: 4, y: 4, z: 4, core: 2. Of those that a mesh axis runs over, the one named last changes fastest.
Arguments:
- tokens: bfloat16 [1024, 8192], P(('col', 'depth'), 'row'), may hold values from -6 to 6
- out_grad: bfloat16 [1024, 8192], P(('col', 'depth'), 'row'), may hold values from -6 to 6
- gate_weight: bfloat16 [8192, 14336], P('row', ('col', 'depth')), may hold values from -0.0625 to 0.0625
- up_weight: bfloat16 [8192, 14336], P('row', ('col', 'depth')), may hold values from -0.0625 to 0.0625
- down_weight: bfloat16 [8192, 14336], P('row', ('col', 'depth')), may hold values from -0.046875 to 0.046875
- gate_mask: int32 [128, 224], P('row', ('col', 'depth')), may hold values 0 or 1
- up_mask: int32 [128, 224], P('row', ('col', 'depth')), may hold values 0 or 1
- down_mask: int32 [128, 224], P('row', ('col', 'depth')), may hold values 0 or 1
Outputs:
- output: float32 [1024, 8192], P(('col', 'depth'), 'row')
- in_grad: float32 [1024, 8192], P(('col', 'depth'), 'row')
- gate_grad: float32 [8192, 14336], P('row', ('col', 'depth'))
- up_grad: float32 [8192, 14336], P('row', ('col', 'depth'))
- down_grad: float32 [8192, 14336], P('row', ('col', 'depth'))
All inputs are finite; a program needn't handle non-finite values. No bound on the sum of `gate_mask` or of `up_mask` or of `down_mask` on one device may be relied on, other than what follows from the above.
Results may differ from a plain program's by a relative error of at most 0.0029.
Values may be sent and summed in bfloat16 or wider, within the bound.
No kernel may reach another device: no remote copies, remote signals or barrier semaphores. Data moves between devices by JAX's collectives and lax.ppermute only.
A program may use at most 192 MiB of HBM per device.

v0:
```python
import functools

import jax
import jax.numpy as jnp
from jax import lax
from jax.experimental import pallas as pl
from jax.experimental.pallas import tpu as pltpu
from jax.sharding import PartitionSpec as P


BF16 = jnp.bfloat16
F16 = jnp.float16
F32 = jnp.float32
SIDE = 4
SCALE = 16.0
MIB = 1 << 20


def send(values, axis, shift):
    if axis == "core":
        return lax.ppermute(values, "depth", [(0, 1), (1, 0)])
    if axis == "z":
        return lax.ppermute(values, "col", [(z, (z + shift) % SIDE) for z in range(SIDE)])
    perm = []
    for y in range(SIDE):
        for x in range(SIDE):
            for core in range(2):
                along_x = (core == 0) == (axis == "first")
                to_y, to_x = (y, (x + shift) % SIDE) if along_x else ((y + shift) % SIDE, x)
                perm.append(((y * SIDE + x) * 2 + core, (to_y * SIDE + to_x) * 2 + core))
    return lax.ppermute(values, ("row", "depth"), perm)


def row_mask(mask, width, first, block):
    rows = lax.broadcasted_iota(jnp.int32, (mask.shape[1], width), 0)
    cols = lax.broadcasted_iota(jnp.int32, (mask.shape[1], width), 1) + first
    spread = jnp.logical_and(cols >= rows * block, cols < (rows + 1) * block).astype(F32)
    return jnp.dot(mask.astype(F32), spread, preferred_element_type=F32)


def mask_kernel(block, count, *refs):
    masks, weights, out, (held, wide, small, came, left, sems) = refs[:count], refs[count:-7], refs[-7], refs[-6:]
    rows, width = weights[0].shape
    copies = [pltpu.make_async_copy(mask, small.at[j], sems.at[j]) for j, mask in enumerate(masks)]
    for copy in copies:
        copy.start()

    def read(i, j):
        at = pl.ds(pl.multiple_of(i * block, block), block)
        return pltpu.make_async_copy(weights[j].at[at, :], held.at[j, at, :], came.at[j, i])

    def write(i, j):
        at = pl.ds(pl.multiple_of(i * block, block), block)
        return pltpu.make_async_copy(held.at[j, at, :], out.at[at, pl.ds(j * width, width)], left.at[j, i])

    def every(act):
        @pl.loop(0, rows // block)
        def _(i):
            for j in range(count):
                act(i, j)

    every(lambda i, j: read(i, j).start())
    for j, copy in enumerate(copies):
        copy.wait()
        wide[j] = row_mask(small[j], width, 0, block)

    def apply(i, j):
        read(i, j).wait()
        at = pl.ds(pl.multiple_of(i * block, block), block)
        held[j, at, :] = (held[j, at, :].astype(F32) * wide[j, pl.ds(i, 1), :]).astype(BF16)
        write(i, j).start()

    every(apply)
    every(lambda i, j: write(i, j).wait())


def mask_weights(weights, masks, vmem):
    rows, width = weights[0].shape
    count, blocks = len(weights), masks[0].shape[0]
    return pl.pallas_call(
        functools.partial(mask_kernel, rows // blocks, count),
        in_specs=[pl.BlockSpec(memory_space=pl.ANY)] * (2 * count),
        out_specs=pl.BlockSpec(memory_space=pl.ANY),
        out_shape=jax.ShapeDtypeStruct((rows, count * width), BF16),
        scratch_shapes=[
            pltpu.VMEM((count, rows, width), BF16),
            pltpu.VMEM((count, blocks, width), F32),
            pltpu.VMEM((count,) + masks[0].shape, jnp.int32),
            pltpu.SemaphoreType.DMA((count, blocks)),
            pltpu.SemaphoreType.DMA((count, blocks)),
            pltpu.SemaphoreType.DMA((count,)),
        ],
        compiler_params=pltpu.CompilerParams(vmem_limit_bytes=vmem * MIB),
    )(*masks, *weights)


def token_row(near, far):
    row, core = lax.axis_index("row"), lax.axis_index("depth")
    y, x = row // SIDE, lax.rem(row, SIDE)
    to_x = lax.rem(x + jnp.where(core == 0, near, far), SIDE)
    to_y = lax.rem(y + jnp.where(core == 0, far, near), SIDE)
    return pl.multiple_of((to_x * SIDE + to_y) * 8, 8)


def roll_kernel(*refs):
    half = len(refs) // 2
    for i in range(16):
        start = token_row(i // SIDE, i % SIDE)
        for j in range(half):
            refs[half + j][pl.ds(i * 8, 8), :] = refs[j][pl.ds(start, 8), :]


def roll_own(*arrays):
    whole = pl.BlockSpec(memory_space=pltpu.VMEM)
    return pl.pallas_call(
        roll_kernel,
        in_specs=[whole] * len(arrays),
        out_specs=[whole] * len(arrays),
        out_shape=[jax.ShapeDtypeStruct(a.shape, a.dtype) for a in arrays],
        compiler_params=pltpu.CompilerParams(vmem_limit_bytes=60 * MIB),
        name="roll_own",
    )(*arrays)


def unroll_kernel(count, *refs):
    owns, got, outs = refs[:count], refs[count:-count], refs[-count:]
    for j, (own, out) in enumerate(zip(owns, outs)):
        width = own.shape[1]
        total = own[...]
        for ref in got:
            total = total + ref[:, pl.ds(j * width, width)].astype(F32)
        for i in range(16):
            out[pl.ds(token_row(i // SIDE, i % SIDE), 8), :] = total[i * 8:(i + 1) * 8]


def unroll_sum(owns, got):
    whole = pl.BlockSpec(memory_space=pltpu.VMEM)
    return pl.pallas_call(
        functools.partial(unroll_kernel, len(owns)),
        in_specs=[whole] * (len(owns) + len(got)),
        out_specs=[whole] * len(owns),
        out_shape=[jax.ShapeDtypeStruct(own.shape, F32) for own in owns],
        compiler_params=pltpu.CompilerParams(vmem_limit_bytes=6 * MIB),
        name="unroll_sum",
    )(*owns, *got)


def place_kernel(*refs):
    *pieces, out, sems = refs
    copies = []
    for i, piece in enumerate(pieces):
        if i < SIDE:
            copies.append(pltpu.make_async_copy(piece, out.at[:, :, i], sems.at[i]))
            continue
        for near in range(SIDE):
            at = sems.at[SIDE + (i - SIDE) * SIDE + near]
            copies.append(pltpu.make_async_copy(piece.at[:, near], out.at[near, :, i], at))
    for copy in copies:
        copy.start()
    for copy in copies:
        copy.wait()


def place_tokens(pieces):
    features = pieces[0].shape[1]
    out = pl.pallas_call(
        place_kernel,
        in_specs=[pl.BlockSpec(memory_space=pl.ANY)] * len(pieces),
        out_specs=pl.BlockSpec(memory_space=pl.ANY),
        out_shape=jax.ShapeDtypeStruct((SIDE, SIDE, len(pieces), 8, features), BF16),
        scratch_shapes=[pltpu.SemaphoreType.DMA((SIDE + SIDE * SIDE,))],
        compiler_params=pltpu.CompilerParams(vmem_limit_bytes=MIB),
    )(*[p.reshape(SIDE, SIDE, 8, features) for p in pieces])
    return out.reshape(128 * len(pieces), features)


def masked_store(out, grad, mask, first, block):
    wide = row_mask(mask, out.shape[1], first, block)
    for i in range(mask.shape[0]):
        at = pl.ds(i * block, block)
        out[at, :] = grad[i * block:(i + 1) * block] * wide[i:i + 1]


def grads_kernel(n_pieces, n_terms, block, *refs):
    take = iter(refs)
    flipped = next(take)
    terms = [[next(take) for _ in range(n_pieces)] for _ in range(n_terms)]
    masks = [next(take) for _ in range(n_terms)]
    outs = [next(take) for _ in range(n_terms)]
    (joined,) = take
    step = pl.program_id(0)

    for pieces, mask, out in zip(terms, masks, outs):
        at = 0
        for piece in pieces:
            joined[pl.ds(at, piece.shape[0]), :] = piece[...]
            at += piece.shape[0]
        grad = jnp.dot(flipped[...], joined[...], preferred_element_type=F32)
        masked_store(out, grad, mask[...], step * out.shape[1], block)


def flip_kernel(tokens, out):
    @pl.loop(0, tokens.shape[0] // 128)
    def _(i):
        at = pl.ds(pl.multiple_of(i * 128, 128), 128)
        out[:, at] = tokens[at, :].T


def flip(tokens):
    return pl.pallas_call(
        flip_kernel,
        in_specs=[pl.BlockSpec(memory_space=pltpu.VMEM)],
        out_specs=pl.BlockSpec(memory_space=pltpu.VMEM),
        out_shape=jax.ShapeDtypeStruct(tokens.shape[::-1], tokens.dtype),
        compiler_params=pltpu.CompilerParams(vmem_limit_bytes=6 * MIB),
    )(tokens)


def weight_grads(flipped, pieces, masks, wide=256):
    features, total = flipped.shape
    n_terms = len(masks)
    width = pieces[0].shape[1] // n_terms
    steps = width // wide
    whole = pl.BlockSpec(memory_space=pltpu.VMEM)
    block = features // masks[0].shape[0]
    term_specs = [
        pl.BlockSpec((piece.shape[0], wide), functools.partial(lambda at, f: (0, at + f), term * steps))
        for term in range(n_terms)
        for piece in pieces
    ]
    return pl.pallas_call(
        functools.partial(grads_kernel, len(pieces), n_terms, block),
        grid=(steps,),
        in_specs=[whole] + term_specs + [whole] * n_terms,
        out_specs=[pl.BlockSpec((features, wide), lambda f: (0, f))] * n_terms,
        out_shape=[jax.ShapeDtypeStruct((features, width), F32)] * n_terms,
        scratch_shapes=[pltpu.VMEM((total, wide), BF16)],
        compiler_params=pltpu.CompilerParams(vmem_limit_bytes=24 * MIB),
    )(flipped, *(list(pieces) * n_terms), *masks)


def partial(tokens, weight):
    return jnp.dot(tokens, weight, preferred_element_type=F32) * SCALE


def sum_first(tokens, weight):
    from_left = send(partial(tokens[384:640], weight).astype(F16), "first", 1)
    from_right = send(partial(tokens[640:896], weight).astype(F16), "first", -1)
    low = (partial(tokens[256:384], weight) + from_left[128:].astype(F32)).astype(F16)
    low_left = send(low, "first", 1)
    high = (partial(tokens[896:], weight) + from_right[:128].astype(F32)).astype(F16)
    high_right = send(high, "first", -1)
    low = partial(tokens[:128], weight) + from_right[128:].astype(F32) + low_left.astype(F32)
    low = low.astype(F16)
    high = partial(tokens[128:256], weight) + from_left[:128].astype(F32) + high_right.astype(F32)
    high = high.astype(F16)
    return low, high


def sum_second(low, high):
    got = [send(values, "second", shift) for shift, values in ((1, low[64:]), (3, high[64:]), (2, high[:64]))]
    total = low[:64].astype(F32)
    for values in got:
        total = total + values.astype(F32)
    return total * (1.0 / SCALE)


def gather_second(values):
    got = {shift: send(values, "second", -shift) for shift in (1, 3, 2)}
    return jnp.concatenate([values, got[1]], axis=0), jnp.concatenate([got[2], got[3]], axis=0)


def gather_first(low, high):
    mine = jnp.concatenate([low, high], axis=0)
    left, right = send(mine, "first", 1), send(mine, "first", -1)
    far_low = send(left[:128], "first", 1)
    far_high = send(right[128:], "first", -1)
    return [mine, right, far_low, far_high, left]


def gather_first_halves(low, high):
    left_low, right_high = send(low, "first", 1), send(high, "first", -1)
    left_high, right_low = send(high, "first", 1), send(low, "first", -1)
    far_low = send(left_low, "first", 1)
    far_high = send(right_high, "first", -1)
    return [low, high, right_low, right_high, far_low, far_high, left_low, left_high]


def gather_tokens(own):
    mine = {0: own}
    for shift in (1, 3, 2):
        mine[shift] = send(own, "z", -shift)
    theirs = {shift: send(mine[shift], "core", 1) for shift in (0, 1, 3, 2)}
    return place_tokens([mine[i] for i in range(SIDE)] + [theirs[i] for i in range(SIDE)])


def chip_kernel(sizes, *refs):
    count = len(sizes)
    mine, theirs, (own, *outs), (kept, came, sems) = refs[:count], refs[count:2 * count], refs[2 * count:-3], refs[-3:]
    copies = []
    at = 0
    for i, size in enumerate(sizes):
        to = pl.ds(at, size)
        copies.append(pltpu.make_async_copy(mine[i].at[:, 0], kept.at[to], sems.at[0, i]))
        copies.append(pltpu.make_async_copy(theirs[i].at[:, 1], came.at[to], sems.at[1, i]))
        at += size
    for copy in copies:
        copy.start()
    for copy in copies:
        copy.wait()

    @pl.loop(0, SIDE)
    def _(near):
        for far in range(SIDE):
            total = kept[near * SIDE + far] + came[far * SIDE + near]
            at = pl.ds(pl.multiple_of((near * SIDE + far) * 8, 8), 8)
            own[at, :] = total[:8]
            for z, out in enumerate(outs):
                out[at, :] = total[(z + 1) * 8:(z + 2) * 8].astype(BF16)


def chip_sum(mine, theirs):
    features = mine[0].shape[1]
    sizes = tuple(p.shape[0] // 64 for p in mine)
    shape = (sum(p.shape[0] for p in mine) // 8, features)
    whole = pl.BlockSpec(memory_space=pltpu.VMEM)
    return pl.pallas_call(
        functools.partial(chip_kernel, sizes),
        in_specs=[pl.BlockSpec(memory_space=pl.ANY)] * (2 * len(sizes)),
        out_specs=[whole] * SIDE,
        out_shape=[jax.ShapeDtypeStruct(shape, F32)] + [jax.ShapeDtypeStruct(shape, BF16)] * (SIDE - 1),
        scratch_shapes=[pltpu.VMEM((16, 32, features), F32)] * 2 + [pltpu.SemaphoreType.DMA((2, len(sizes)))],
        compiler_params=pltpu.CompilerParams(vmem_limit_bytes=6 * MIB),
        name="chip_sum",
    )(*[p.reshape(-1, 2, 32, features) for p in (*mine, *theirs)])


def back_product(groups, weights):
    mine, theirs = [], []
    for pieces in groups:
        parts = [
            lax.dot_general(p, weights, (((1,), (1,)), ((), ())), preferred_element_type=F32) for p in pieces
        ]
        mine.append(jnp.concatenate(parts, axis=0))
        theirs.append(send(mine[-1], "core", 1))
    return chip_sum(mine, theirs)


def per_device(
    tokens, out_grad, gate_weight, up_weight, down_weight, gate_mask, up_mask, down_mask
):
    tokens, out_grad = roll_own(tokens, out_grad)
    w_gate_up = mask_weights((gate_weight, up_weight), (gate_mask, up_mask), 54)
    w_down = mask_weights((down_weight,), (down_mask,), 40)
    width = w_down.shape[1]

    ins = gather_tokens(tokens)
    outs = gather_tokens(out_grad)
    near_gate_up = sum_first(ins, w_gate_up)
    near_grad = sum_first(outs, w_down)

    gate_up = sum_second(*near_gate_up)
    gate, up = gate_up[:, :width], gate_up[:, width:]
    hidden = gather_first(*gather_second((gate * jax.nn.sigmoid(gate) * up).astype(BF16)))

    grad = sum_second(*near_grad)
    gate, up, grad = lax.optimization_barrier((gate, up, grad))
    sig = jax.nn.sigmoid(gate)
    act = gate * sig
    gate_term = (grad * up * sig * (1.0 + gate * (1.0 - sig))).astype(BF16)
    up_term = (grad * act).astype(BF16)
    terms = gather_second(jnp.concatenate([gate_term, up_term], axis=1))
    terms = gather_first_halves(*terms)

    outs_flipped = flip(outs)
    ins_flipped = flip(ins)

    ys = back_product([hidden], w_down)
    (down_grad,) = weight_grads(outs_flipped, hidden, [down_mask])
    dxs = back_product([terms[i:i + 2] for i in range(0, 8, 2)], w_gate_up)
    gate_grad, up_grad = weight_grads(ins_flipped, terms, [gate_mask, up_mask])
    got = [send(jnp.concatenate([ys[z], dxs[z]], axis=1), "z", z) for z in (1, 3, 2)]
    output, in_grad = unroll_sum((ys[0], dxs[0]), got)
    return (output, in_grad, gate_grad, up_grad, down_grad)


def solution(mesh):
    data, weight = P(("col", "depth"), "row"), P("row", ("col", "depth"))

    return jax.shard_map(
        per_device,
        mesh=mesh,
        in_specs=(data,) * 2 + (weight,) * 6,
        out_specs=(data,) * 2 + (weight,) * 3,
        check_vma=False,
    )
```

profile of v0, /device:TPU:0, one launch (start us, length us, event | category | flops | bytes accessed | tf_op | source)
XLA Modules:
  0.0 215.9 jit_solution(9798311993665577317)
XLA Ops:
  2.4 4.1 %collective-permute-start = (bf16[128,512]{1,0:T(8,128)(2,1)}, bf16[128,512]{1,0:T(8,128)(2,1)S(1)}, u32[]{:S(2)}, u32[]{:S(2)}) collective-permute-start(bf16[128,512]{1,0:T(8,128)(2,1)} %get-tuple-element.22), channel_id=1, source_target_pairs={{0,6},{2,0},{4,2},{6,4},{1,7},{3,1},{5,3},{7,5},{8,14},{10,8},{12,... | collective-permute-start | bytes 393224 | tf_op jit(solution)/shard_map/ppermute | solution.py:23
  7.1 3.0 %collective-permute-start.23 = (bf16[128,512]{1,0:T(8,128)(2,1)}, bf16[128,512]{1,0:T(8,128)(2,1)S(1)}, u32[]{:S(2)}, u32[]{:S(2)}) collective-permute-start(bf16[128,512]{1,0:T(8,128)(2,1)} %get-tuple-element.24), channel_id=1, source_target_pairs={{0,4},{2,6},{4,0},{6,2},{1,5},{3,7},{5,1},{7,3},{8,12},{10,14},{12... | collective-permute-start | bytes 393224 | tf_op jit(solution)/shard_map/ppermute | solution.py:23
  11.5 2.4 %collective-permute-done = bf16[128,512]{1,0:T(8,128)(2,1)S(1)} collective-permute-done((bf16[128,512]{1,0:T(8,128)(2,1)}, bf16[128,512]{1,0:T(8,128)(2,1)S(1)}, u32[]{:S(2)}, u32[]{:S(2)}) %collective-permute-start) | collective-permute-done | bytes 131104 | tf_op jit(solution)/shard_map/ppermute | solution.py:23
  14.7 3.3 %collective-permute-done.22 = bf16[128,512]{1,0:T(8,128)(2,1)S(1)} collective-permute-done((bf16[128,512]{1,0:T(8,128)(2,1)}, bf16[128,512]{1,0:T(8,128)(2,1)S(1)}, u32[]{:S(2)}, u32[]{:S(2)}) %collective-permute-start.22) | collective-permute-done | bytes 131104 | tf_op jit(solution)/shard_map/ppermute | solution.py:23
  21.2 5.5 %shard_map.121 = bf16[512,1792]{1,0:T(8,128)(2,1)S(1)} custom-call(s32[8,28]{1,0:T(8,128)S(1)} %copy-done.5, bf16[512,1792]{1,0:T(8,128)(2,1)S(1)} %copy-done), custom_call_target="tpu_custom_call" | custom-call | tf_op jit(solution)/shard_map/pallas_call | solution.py:80
  29.1 2.8 %collective-permute-start.29 = (f16[256,1792]{1,0:T(8,128)(2,1)S(1)}, f16[256,1792]{1,0:T(8,128)(2,1)S(1)}, u32[]{:S(2)}, u32[]{:S(2)}) collective-permute-start(f16[256,1792]{1,0:T(8,128)(2,1)S(1)} %fusion.12), channel_id=1, source_target_pairs={{0,24},{1,97},{8,0},{9,105},{16,8},{17,113},{24,16},{25,121},{32,5... | collective-permute-start | bytes 2752520 | tf_op jit(solution)/shard_map/ppermute | solution.py:31
  31.9 3.7 %shard_map.120 = bf16[512,3584]{1,0:T(8,128)(2,1)} custom-call(s32[8,28]{1,0:T(8,128)} %refs_17_.1, s32[8,28]{1,0:T(8,128)} %refs_18_.1, bf16[512,1792]{1,0:T(8,128)(2,1)} %refs_2_.1, bf16[512,1792]{1,0:T(8,128)(2,1)} %refs_3_.1), custom_call_target="tpu_custom_call" | custom-call | tf_op jit(solution)/shard_map/pallas_call | solution.py:80
  36.1 3.2 %fusion = f16[256,3584]{1,0:T(8,128)(2,1)S(1)} fusion(bf16[512,3584]{1,0:T(8,128)(2,1)} %shard_map.120, bf16[1024,512]{1,0:T(8,128)(2,1)S(1)} %bitcast.64), kind=kOutput, calls=%fused_computation.2 | convolution fusion | flops 941359104 | bytes 5767168 | tf_op jit(solution)/shard_map/dot_general | solution.py:243
  43.2 3.8 %collective-permute-start.33 = (f16[128,1792]{1,0:T(8,128)(2,1)S(1)}, f16[128,1792]{1,0:T(8,128)(2,1)S(1)}, u32[]{:S(2)}, u32[]{:S(2)}) collective-permute-start(f16[128,1792]{1,0:T(8,128)(2,1)S(1)} %fusion.21), channel_id=1, source_target_pairs={{0,24},{1,97},{8,0},{9,105},{16,8},{17,113},{24,16},{25,121},{32,5... | collective-permute-start | bytes 1376264 | tf_op jit(solution)/shard_map/ppermute | solution.py:31
  48.2 7.3 %collective-permute-done.30 = f16[256,1792]{1,0:T(8,128)(2,1)S(1)} collective-permute-done((f16[256,1792]{1,0:T(8,128)(2,1)S(1)}, f16[256,1792]{1,0:T(8,128)(2,1)S(1)}, u32[]{:S(2)}, u32[]{:S(2)}) %collective-permute-start.30) | collective-permute-done | bytes 917536 | tf_op jit(solution)/shard_map/ppermute | solution.py:31
  56.2 11.3 %collective-permute-done.33 = f16[128,1792]{1,0:T(8,128)(2,1)S(1)} collective-permute-done((f16[128,1792]{1,0:T(8,128)(2,1)S(1)}, f16[128,1792]{1,0:T(8,128)(2,1)S(1)}, u32[]{:S(2)}, u32[]{:S(2)}) %collective-permute-start.33) | collective-permute-done | bytes 458784 | tf_op jit(solution)/shard_map/ppermute | solution.py:31
  68.7 3.7 %collective-permute-start.11 = (f16[128,3584]{1,0:T(8,128)(2,1)S(1)}, f16[128,3584]{1,0:T(8,128)(2,1)S(1)}, u32[]{:S(2)}, u32[]{:S(2)}) collective-permute-start(f16[128,3584]{1,0:T(8,128)(2,1)S(1)} %fusion.11), channel_id=1, source_target_pairs={{0,24},{1,97},{8,0},{9,105},{16,8},{17,113},{24,16},{25,121},{32,5... | collective-permute-start | bytes 2752520 | tf_op jit(solution)/shard_map/ppermute | solution.py:31
  72.4 3.3 %collective-permute-start.35 = (f16[64,1792]{1,0:T(8,128)(2,1)S(1)}, f16[64,1792]{1,0:T(8,128)(2,1)S(1)}, u32[]{:S(2)}, u32[]{:S(2)}) collective-permute-start(f16[64,1792]{1,0:T(8,128)(2,1)S(1)} %get-tuple-element.47), channel_id=1, source_target_pairs={{0,64},{1,17},{8,72},{9,25},{16,80},{17,1},{24,88},{25,9},{32,96},... | collective-permute-start | bytes 688136 | tf_op jit(solution)/shard_map/ppermute | solution.py:31
  76.7 5.8 %collective-permute-done.31 = f16[128,1792]{1,0:T(8,128)(2,1)S(1)} collective-permute-done((f16[128,1792]{1,0:T(8,128)(2,1)S(1)}, f16[128,1792]{1,0:T(8,128)(2,1)S(1)}, u32[]{:S(2)}, u32[]{:S(2)}) %collective-permute-start.31) | collective-permute-done | bytes 458784 | tf_op jit(solution)/shard_map/ppermute | solution.py:31
  85.5 2.7 %collective-permute-done.11 = f16[128,3584]{1,0:T(8,128)(2,1)S(1)} collective-permute-done((f16[128,3584]{1,0:T(8,128)(2,1)S(1)}, f16[128,3584]{1,0:T(8,128)(2,1)S(1)}, u32[]{:S(2)}, u32[]{:S(2)}) %collective-permute-start.11) | collective-permute-done | bytes 917536 | tf_op jit(solution)/shard_map/ppermute | solution.py:31
  89.1 2.1 collective-permute-start.13
  91.3 13.7 %collective-permute-done.9 = f16[128,3584]{1,0:T(8,128)(2,1)S(1)} collective-permute-done((f16[128,3584]{1,0:T(8,128)(2,1)S(1)}, f16[128,3584]{1,0:T(8,128)(2,1)S(1)}, u32[]{:S(2)}, u32[]{:S(2)}) %collective-permute-start.9) | collective-permute-done | bytes 917536 | tf_op jit(solution)/shard_map/ppermute | solution.py:31
  108.2 5.3 %collective-permute-done.12 = f16[64,3584]{1,0:T(8,128)(2,1)S(1)} collective-permute-done((f16[64,3584]{1,0:T(8,128)(2,1)S(1)}, f16[64,3584]{1,0:T(8,128)(2,1)S(1)}, u32[]{:S(2)}, u32[]{:S(2)}) %collective-permute-start.12) | collective-permute-done | bytes 458784 | tf_op jit(solution)/shard_map/ppermute | solution.py:31
  113.5 3.8 %collective-permute-done.10 = f16[64,3584]{1,0:T(8,128)(2,1)S(1)} collective-permute-done((f16[64,3584]{1,0:T(8,128)(2,1)S(1)}, f16[64,3584]{1,0:T(8,128)(2,1)S(1)}, u32[]{:S(2)}, u32[]{:S(2)}) %collective-permute-start.10) | collective-permute-done | bytes 458784 | tf_op jit(solution)/shard_map/ppermute | solution.py:31
  117.9 2.0 collective-permute-start.15
  121.9 2.6 %collective-permute-start.37 = (bf16[64,3584]{1,0:T(8,128)(2,1)S(1)}, bf16[64,3584]{1,0:T(8,128)(2,1)S(1)}, u32[]{:S(2)}, u32[]{:S(2)}) collective-permute-start(bf16[64,3584]{1,0:T(8,128)(2,1)S(1)} %pad_maximum_fusion.6), channel_id=1, source_target_pairs={{0,64},{1,17},{8,72},{9,25},{16,80},{17,1},{24,88},{25,9},{32,96},... | collective-permute-start | bytes 1376264 | tf_op jit(solution)/shard_map/ppermute | solution.py:31
  124.4 7.7 %collective-permute-done.16 = bf16[64,1792]{1,0:T(8,128)(2,1)S(1)} collective-permute-done((bf16[64,1792]{1,0:T(8,128)(2,1)S(1)}, bf16[64,1792]{1,0:T(8,128)(2,1)S(1)}, u32[]{:S(2)}, u32[]{:S(2)}) %collective-permute-start.16) | collective-permute-done | bytes 229408 | tf_op jit(solution)/shard_map/ppermute | solution.py:31
  135.0 6.5 %collective-permute-done.38 = bf16[64,3584]{1,0:T(8,128)(2,1)S(1)} collective-permute-done((bf16[64,3584]{1,0:T(8,128)(2,1)S(1)}, bf16[64,3584]{1,0:T(8,128)(2,1)S(1)}, u32[]{:S(2)}, u32[]{:S(2)}) %collective-permute-start.38) | collective-permute-done | bytes 458784 | tf_op jit(solution)/shard_map/ppermute | solution.py:31
  141.6 3.9 %collective-permute-done.36 = bf16[64,3584]{1,0:T(8,128)(2,1)S(1)} collective-permute-done((bf16[64,3584]{1,0:T(8,128)(2,1)S(1)}, bf16[64,3584]{1,0:T(8,128)(2,1)S(1)}, u32[]{:S(2)}, u32[]{:S(2)}) %collective-permute-start.36) | collective-permute-done | bytes 458784 | tf_op jit(solution)/shard_map/ppermute | solution.py:31
  151.5 4.9 %collective-permute-done.40.refs_4_.refs_12_ = bf16[128,3584]{1,0:T(8,128)(2,1)S(1)} collective-permute-done((bf16[128,3584]{1,0:T(8,128)(2,1)S(1)}, bf16[128,3584]{1,0:T(8,128)(2,1)S(1)}, u32[]{:S(2)}, u32[]{:S(2)}) %collective-permute-start.40) | collective-permute-done | bytes 917536 | tf_op jit(solution)/shard_map/ppermute | solution.py:31
  157.7 4.2 %collective-permute-done.41.refs_7_.refs_15_ = bf16[128,3584]{1,0:T(8,128)(2,1)S(1)} collective-permute-done((bf16[128,3584]{1,0:T(8,128)(2,1)S(1)}, bf16[128,3584]{1,0:T(8,128)(2,1)S(1)}, u32[]{:S(2)}, u32[]{:S(2)}) %collective-permute-start.41) | collective-permute-done | bytes 917536 | tf_op jit(solution)/shard_map/ppermute | solution.py:31
  163.2 13.5 %collective-permute-done.19.refs_3_ = bf16[128,1792]{1,0:T(8,128)(2,1)S(1)} collective-permute-done((bf16[128,1792]{1,0:T(8,128)(2,1)S(1)}, bf16[128,1792]{1,0:T(8,128)(2,1)S(1)}, u32[]{:S(2)}, u32[]{:S(2)}) %collective-permute-start.19) | collective-permute-done | bytes 458784 | tf_op jit(solution)/shard_map/ppermute | solution.py:31
  177.4 2.1 collective-permute-start.42
  184.2 5.8 %collective-permute-done.43.refs_6_.refs_14_ = bf16[128,3584]{1,0:T(8,128)(2,1)S(1)} collective-permute-done((bf16[128,3584]{1,0:T(8,128)(2,1)S(1)}, bf16[128,3584]{1,0:T(8,128)(2,1)S(1)}, u32[]{:S(2)}, u32[]{:S(2)}) %collective-permute-start.43) | collective-permute-done | bytes 917536 | tf_op jit(solution)/shard_map/ppermute | solution.py:31
  196.9 2.5 %collective-permute-start.50 = (bf16[128,1024]{1,0:T(8,128)(2,1)S(1)}, bf16[128,1024]{1,0:T(8,128)(2,1)S(1)}, u32[]{:S(2)}, u32[]{:S(2)}) collective-permute-start(bf16[128,1024]{1,0:T(8,128)(2,1)S(1)} %pad_maximum_fusion.8), channel_id=1, source_target_pairs={{0,6},{2,0},{4,2},{6,4},{1,7},{3,1},{5,3},{7,5},{8,14},{10,8},{12,... | collective-permute-start | bytes 786440 | tf_op jit(solution)/shard_map/ppermute | solution.py:23
  202.4 5.3 %shard_map.126 = f32[512,1792]{1,0:T(8,128)} custom-call(bf16[512,1024]{1,0:T(8,128)(2,1)S(1)} %shard_map.125.refs_0_, bf16[256,1792]{1,0:T(8,128)(2,1)S(1)} %pad_maximum_fusion.refs_1_, bf16[256,1792]{1,0:T(8,128)(2,1)S(1)} %collective-permute-done.17.refs_2_, bf16[128,1792]{1,0:T(8,128)(2,1)S(1)} %collective-permute-done.19.refs_3_, ...), custom_call_target="tpu_custom_call" | custom-call | tf_op jit(solution)/shard_map/pallas_call | solution.py:231
  207.7 7.2 %shard_map.124 = (f32[512,1792]{1,0:T(8,128)}, f32[512,1792]{1,0:T(8,128)}) custom-call(bf16[512,1024]{1,0:T(8,128)(2,1)S(1)} %shard_map.123.refs_0_, bf16[128,3584]{1,0:T(8,128)(2,1)S(1)} %pad_maximum_fusion.1.refs_1_.refs_9_, bf16[128,3584]{1,0:T(8,128)(2,1)S(1)} %constant_dynamic-update-slice_fusion.refs_2_.refs_10_, ...), custom_call_target="tpu_custom_call" | custom-call | tf_op jit(solution)/shard_map/pallas_call | solution.py:231
  (147 shorter events, 55.7 us)
Async XLA Ops:
  29.1 13.7 %collective-permute-start.29 = (f16[256,1792]{1,0:T(8,128)(2,1)S(1)}, f16[256,1792]{1,0:T(8,128)(2,1)S(1)}, u32[]{:S(2)}, u32[]{:S(2)}) collective-permute-start(f16[256,1792]{1,0:T(8,128)(2,1)S(1)} %fusion.12), channel_id=1, source_target_pairs={{0,24},{1,97},{8,0},{9,105},{16,8},{17,113},{24,16},{25,121},{32,5... | collective-permute-start | bytes 2752520 | tf_op jit(solution)/shard_map/ppermute | solution.py:31
  39.3 28.7 %collective-permute-start.7 = (f16[256,3584]{1,0:T(8,128)(2,1)S(1)}, f16[256,3584]{1,0:T(8,128)(2,1)S(1)}, u32[]{:S(2)}, u32[]{:S(2)}) collective-permute-start(f16[256,3584]{1,0:T(8,128)(2,1)S(1)} %fusion), channel_id=1, source_target_pairs={{0,24},{1,97},{8,0},{9,105},{16,8},{17,113},{24,16},{25,121},{32,5... | collective-permute-start | bytes 5505032 | tf_op jit(solution)/shard_map/ppermute | solution.py:31
  40.8 14.7 %collective-permute-start.30 = (f16[256,1792]{1,0:T(8,128)(2,1)S(1)}, f16[256,1792]{1,0:T(8,128)(2,1)S(1)}, u32[]{:S(2)}, u32[]{:S(2)}) collective-permute-start(f16[256,1792]{1,0:T(8,128)(2,1)S(1)} %fusion.13), channel_id=1, source_target_pairs={{0,8},{1,33},{8,16},{9,41},{16,24},{17,49},{24,0},{25,57},{32,40},... | collective-permute-start | bytes 2752520 | tf_op jit(solution)/shard_map/ppermute | solution.py:31
  43.2 24.2 %collective-permute-start.33 = (f16[128,1792]{1,0:T(8,128)(2,1)S(1)}, f16[128,1792]{1,0:T(8,128)(2,1)S(1)}, u32[]{:S(2)}, u32[]{:S(2)}) collective-permute-start(f16[128,1792]{1,0:T(8,128)(2,1)S(1)} %fusion.21), channel_id=1, source_target_pairs={{0,24},{1,97},{8,0},{9,105},{16,8},{17,113},{24,16},{25,121},{32,5... | collective-permute-start | bytes 1376264 | tf_op jit(solution)/shard_map/ppermute | solution.py:31
  48.1 36.5 %collective-permute-start.8 = (f16[256,3584]{1,0:T(8,128)(2,1)S(1)}, f16[256,3584]{1,0:T(8,128)(2,1)S(1)}, u32[]{:S(2)}, u32[]{:S(2)}) collective-permute-start(f16[256,3584]{1,0:T(8,128)(2,1)S(1)} %fusion.1), channel_id=1, source_target_pairs={{0,8},{1,33},{8,16},{9,41},{16,24},{17,49},{24,0},{25,57},{32,40},... | collective-permute-start | bytes 5505032 | tf_op jit(solution)/shard_map/ppermute | solution.py:31
  55.9 26.6 %collective-permute-start.31 = (f16[128,1792]{1,0:T(8,128)(2,1)S(1)}, f16[128,1792]{1,0:T(8,128)(2,1)S(1)}, u32[]{:S(2)}, u32[]{:S(2)}) collective-permute-start(f16[128,1792]{1,0:T(8,128)(2,1)S(1)} %fusion.20), channel_id=1, source_target_pairs={{0,8},{1,33},{8,16},{9,41},{16,24},{17,49},{24,0},{25,57},{32,40},... | collective-permute-start | bytes 1376264 | tf_op jit(solution)/shard_map/ppermute | solution.py:31
  68.7 19.5 %collective-permute-start.11 = (f16[128,3584]{1,0:T(8,128)(2,1)S(1)}, f16[128,3584]{1,0:T(8,128)(2,1)S(1)}, u32[]{:S(2)}, u32[]{:S(2)}) collective-permute-start(f16[128,3584]{1,0:T(8,128)(2,1)S(1)} %fusion.11), channel_id=1, source_target_pairs={{0,24},{1,97},{8,0},{9,105},{16,8},{17,113},{24,16},{25,121},{32,5... | collective-permute-start | bytes 2752520 | tf_op jit(solution)/shard_map/ppermute | solution.py:31
  72.4 35.1 %collective-permute-start.35 = (f16[64,1792]{1,0:T(8,128)(2,1)S(1)}, f16[64,1792]{1,0:T(8,128)(2,1)S(1)}, u32[]{:S(2)}, u32[]{:S(2)}) collective-permute-start(f16[64,1792]{1,0:T(8,128)(2,1)S(1)} %get-tuple-element.47), channel_id=1, source_target_pairs={{0,64},{1,17},{8,72},{9,25},{16,80},{17,1},{24,88},{25,9},{32,96},... | collective-permute-start | bytes 688136 | tf_op jit(solution)/shard_map/ppermute | solution.py:31
  75.7 32.3 %collective-permute-start.34 = (f16[64,1792]{1,0:T(8,128)(2,1)S(1)}, f16[64,1792]{1,0:T(8,128)(2,1)S(1)}, u32[]{:S(2)}, u32[]{:S(2)}) collective-permute-start(f16[64,1792]{1,0:T(8,128)(2,1)S(1)} %get-tuple-element.46), channel_id=1, source_target_pairs={{0,96},{1,25},{8,104},{9,1},{16,112},{17,9},{24,120},{25,17},{32,0... | collective-permute-start | bytes 688136 | tf_op jit(solution)/shard_map/ppermute | solution.py:31
  83.0 24.9 %collective-permute-start.32 = (f16[64,1792]{1,0:T(8,128)(2,1)S(1)}, f16[64,1792]{1,0:T(8,128)(2,1)S(1)}, u32[]{:S(2)}, u32[]{:S(2)}) collective-permute-start(f16[64,1792]{1,0:T(8,128)(2,1)S(1)} %slice.153), channel_id=1, source_target_pairs={{0,32},{1,9},{8,40},{9,17},{16,48},{17,25},{24,56},{25,1},{32,64},... | collective-permute-start | bytes 688136 | tf_op jit(solution)/shard_map/ppermute | solution.py:31
  85.4 19.6 %collective-permute-start.9 = (f16[128,3584]{1,0:T(8,128)(2,1)S(1)}, f16[128,3584]{1,0:T(8,128)(2,1)S(1)}, u32[]{:S(2)}, u32[]{:S(2)}) collective-permute-start(f16[128,3584]{1,0:T(8,128)(2,1)S(1)} %fusion.9), channel_id=1, source_target_pairs={{0,8},{1,33},{8,16},{9,41},{16,24},{17,49},{24,0},{25,57},{32,40},... | collective-permute-start | bytes 2752520 | tf_op jit(solution)/shard_map/ppermute | solution.py:31
  89.1 19.0 %collective-permute-start.13 = (f16[64,3584]{1,0:T(8,128)(2,1)S(1)}, f16[64,3584]{1,0:T(8,128)(2,1)S(1)}, u32[]{:S(2)}, u32[]{:S(2)}) collective-permute-start(f16[64,3584]{1,0:T(8,128)(2,1)S(1)} %get-tuple-element.45), channel_id=1, source_target_pairs={{0,64},{1,17},{8,72},{9,25},{16,80},{17,1},{24,88},{25,9},{32,96},... | collective-permute-start | bytes 1376264 | tf_op jit(solution)/shard_map/ppermute | solution.py:31
  117.8 14.3 %collective-permute-start.16 = (bf16[64,1792]{1,0:T(8,128)(2,1)S(1)}, bf16[64,1792]{1,0:T(8,128)(2,1)S(1)}, u32[]{:S(2)}, u32[]{:S(2)}) collective-permute-start(bf16[64,1792]{1,0:T(8,128)(2,1)S(1)} %get-tuple-element.42), channel_id=1, source_target_pairs={{0,32},{1,9},{8,40},{9,17},{16,48},{17,25},{24,56},{25,1},{32,64},... | collective-permute-start | bytes 688136 | tf_op jit(solution)/shard_map/ppermute | solution.py:31
  117.9 14.3 %collective-permute-start.15 = (bf16[64,1792]{1,0:T(8,128)(2,1)S(1)}, bf16[64,1792]{1,0:T(8,128)(2,1)S(1)}, u32[]{:S(2)}, u32[]{:S(2)}) collective-permute-start(bf16[64,1792]{1,0:T(8,128)(2,1)S(1)} %get-tuple-element.42), channel_id=1, source_target_pairs={{0,64},{1,17},{8,72},{9,25},{16,80},{17,1},{24,88},{25,9},{32,96},... | collective-permute-start | bytes 688136 | tf_op jit(solution)/shard_map/ppermute | solution.py:31
  121.9 13.1 %collective-permute-start.37 = (bf16[64,3584]{1,0:T(8,128)(2,1)S(1)}, bf16[64,3584]{1,0:T(8,128)(2,1)S(1)}, u32[]{:S(2)}, u32[]{:S(2)}) collective-permute-start(bf16[64,3584]{1,0:T(8,128)(2,1)S(1)} %pad_maximum_fusion.6), channel_id=1, source_target_pairs={{0,64},{1,17},{8,72},{9,25},{16,80},{17,1},{24,88},{25,9},{32,96},... | collective-permute-start | bytes 1376264 | tf_op jit(solution)/shard_map/ppermute | solution.py:31
  124.4 17.1 %collective-permute-start.38 = (bf16[64,3584]{1,0:T(8,128)(2,1)S(1)}, bf16[64,3584]{1,0:T(8,128)(2,1)S(1)}, u32[]{:S(2)}, u32[]{:S(2)}) collective-permute-start(bf16[64,3584]{1,0:T(8,128)(2,1)S(1)} %pad_maximum_fusion.6), channel_id=1, source_target_pairs={{0,32},{1,9},{8,40},{9,17},{16,48},{17,25},{24,56},{25,1},{32,64},... | collective-permute-start | bytes 1376264 | tf_op jit(solution)/shard_map/ppermute | solution.py:31
  132.1 13.4 %collective-permute-start.36 = (bf16[64,3584]{1,0:T(8,128)(2,1)S(1)}, bf16[64,3584]{1,0:T(8,128)(2,1)S(1)}, u32[]{:S(2)}, u32[]{:S(2)}) collective-permute-start(bf16[64,3584]{1,0:T(8,128)(2,1)S(1)} %pad_maximum_fusion.6), channel_id=1, source_target_pairs={{0,96},{1,25},{8,104},{9,1},{16,112},{17,9},{24,120},{25,17},{32,0... | collective-permute-start | bytes 1376264 | tf_op jit(solution)/shard_map/ppermute | solution.py:31
  132.2 18.5 %collective-permute-start.17 = (bf16[256,1792]{1,0:T(8,128)(2,1)S(1)}, bf16[256,1792]{1,0:T(8,128)(2,1)S(1)}, u32[]{:S(2)}, u32[]{:S(2)}) collective-permute-start(bf16[256,1792]{1,0:T(8,128)(2,1)S(1)} %pad_maximum_fusion.refs_1_), channel_id=1, source_target_pairs={{0,24},{1,97},{8,0},{9,105},{16,8},{17,113},{24,16},{25,121},{32,5... | collective-permute-start | bytes 2752520 | tf_op jit(solution)/shard_map/ppermute | solution.py:31
  132.3 18.2 %collective-permute-start.18 = (bf16[256,1792]{1,0:T(8,128)(2,1)S(1)}, bf16[256,1792]{1,0:T(8,128)(2,1)S(1)}, u32[]{:S(2)}, u32[]{:S(2)}) collective-permute-start(bf16[256,1792]{1,0:T(8,128)(2,1)S(1)} %pad_maximum_fusion.refs_1_), channel_id=1, source_target_pairs={{0,8},{1,33},{8,16},{9,41},{16,24},{17,49},{24,0},{25,57},{32,40},... | collective-permute-start | bytes 2752520 | tf_op jit(solution)/shard_map/ppermute | solution.py:31
  141.5 14.9 %collective-permute-start.40 = (bf16[128,3584]{1,0:T(8,128)(2,1)S(1)}, bf16[128,3584]{1,0:T(8,128)(2,1)S(1)}, u32[]{:S(2)}, u32[]{:S(2)}) collective-permute-start(bf16[128,3584]{1,0:T(8,128)(2,1)S(1)} %constant_dynamic-update-slice_fusion.refs_2_.refs_10_), channel_id=1, source_target_pairs={{0,24},{1,97},{8,0},{9,105},{16,8},{17,113},{24,16},{25,121},{32,5... | collective-permute-start | bytes 2752520 | tf_op jit(solution)/shard_map/ppermute | solution.py:31
  146.9 34.0 %collective-permute-start.39 = (bf16[128,3584]{1,0:T(8,128)(2,1)S(1)}, bf16[128,3584]{1,0:T(8,128)(2,1)S(1)}, u32[]{:S(2)}, u32[]{:S(2)}) collective-permute-start(bf16[128,3584]{1,0:T(8,128)(2,1)S(1)} %pad_maximum_fusion.1.refs_1_.refs_9_), channel_id=1, source_target_pairs={{0,24},{1,97},{8,0},{9,105},{16,8},{17,113},{24,16},{25,121},{32,5... | collective-permute-start | bytes 2752520 | tf_op jit(solution)/shard_map/ppermute | solution.py:31
  147.2 14.7 %collective-permute-start.41 = (bf16[128,3584]{1,0:T(8,128)(2,1)S(1)}, bf16[128,3584]{1,0:T(8,128)(2,1)S(1)}, u32[]{:S(2)}, u32[]{:S(2)}) collective-permute-start(bf16[128,3584]{1,0:T(8,128)(2,1)S(1)} %pad_maximum_fusion.1.refs_1_.refs_9_), channel_id=1, source_target_pairs={{0,8},{1,33},{8,16},{9,41},{16,24},{17,49},{24,0},{25,57},{32,40},... | collective-permute-start | bytes 2752520 | tf_op jit(solution)/shard_map/ppermute | solution.py:31
  150.6 31.7 %collective-permute-start.44 = (bf16[128,3584]{1,0:T(8,128)(2,1)S(1)}, bf16[128,3584]{1,0:T(8,128)(2,1)S(1)}, u32[]{:S(2)}, u32[]{:S(2)}) collective-permute-start(bf16[128,3584]{1,0:T(8,128)(2,1)S(1)} %constant_dynamic-update-slice_fusion.refs_2_.refs_10_), channel_id=1, source_target_pairs={{0,8},{1,33},{8,16},{9,41},{16,24},{17,49},{24,0},{25,57},{32,40},... | collective-permute-start | bytes 2752520 | tf_op jit(solution)/shard_map/ppermute | solution.py:31
  150.7 42.8 %collective-permute-start.45 = (f32[256,512]{1,0:T(8,128)S(1)}, f32[256,512]{1,0:T(8,128)S(1)}, u32[]{:S(2)}, u32[]{:S(2)}) collective-permute-start(f32[256,512]{1,0:T(8,128)S(1)} %pad_maximum_fusion.2), channel_id=1, source_target_pairs={{0,1},{1,0},{2,3},{3,2},{4,5},{5,4},{6,7},{7,6},{8,9},{9,8},{10,11... | collective-permute-start | bytes 1572872 | tf_op jit(solution)/shard_map/ppermute | solution.py:21
  156.4 20.2 %collective-permute-start.19 = (bf16[128,1792]{1,0:T(8,128)(2,1)S(1)}, bf16[128,1792]{1,0:T(8,128)(2,1)S(1)}, u32[]{:S(2)}, u32[]{:S(2)}) collective-permute-start(bf16[128,1792]{1,0:T(8,128)(2,1)S(1)} %slice.144), channel_id=1, source_target_pairs={{0,8},{1,33},{8,16},{9,41},{16,24},{17,49},{24,0},{25,57},{32,40},... | collective-permute-start | bytes 1376264 | tf_op jit(solution)/shard_map/ppermute | solution.py:31
  161.9 15.5 %collective-permute-start.20 = (bf16[128,1792]{1,0:T(8,128)(2,1)S(1)}, bf16[128,1792]{1,0:T(8,128)(2,1)S(1)}, u32[]{:S(2)}, u32[]{:S(2)}) collective-permute-start(bf16[128,1792]{1,0:T(8,128)(2,1)S(1)} %slice.145), channel_id=1, source_target_pairs={{0,24},{1,97},{8,0},{9,105},{16,8},{17,113},{24,16},{25,121},{32,5... | collective-permute-start | bytes 1376264 | tf_op jit(solution)/shard_map/ppermute | solution.py:31
  176.6 13.4 %collective-permute-start.43 = (bf16[128,3584]{1,0:T(8,128)(2,1)S(1)}, bf16[128,3584]{1,0:T(8,128)(2,1)S(1)}, u32[]{:S(2)}, u32[]{:S(2)}) collective-permute-start(bf16[128,3584]{1,0:T(8,128)(2,1)S(1)} %collective-permute-done.40.refs_4_.refs_12_), channel_id=1, source_target_pairs={{0,24},{1,97},{8,0},{9,105},{16,8},{17,113},{24,16},{25,121},{32,5... | collective-permute-start | bytes 2752520 | tf_op jit(solution)/shard_map/ppermute | solution.py:31
  177.4 14.7 %collective-permute-start.42 = (bf16[128,3584]{1,0:T(8,128)(2,1)S(1)}, bf16[128,3584]{1,0:T(8,128)(2,1)S(1)}, u32[]{:S(2)}, u32[]{:S(2)}) collective-permute-start(bf16[128,3584]{1,0:T(8,128)(2,1)S(1)} %collective-permute-done.41.refs_7_.refs_15_), channel_id=1, source_target_pairs={{0,8},{1,33},{8,16},{9,41},{16,24},{17,49},{24,0},{25,57},{32,40},... | collective-permute-start | bytes 2752520 | tf_op jit(solution)/shard_map/ppermute | solution.py:31
  180.9 14.8 %collective-permute-start.21 = (f32[1024,512]{1,0:T(8,128)S(1)}, f32[1024,512]{1,0:T(8,128)S(1)}, u32[]{:S(2)}, u32[]{:S(2)}) collective-permute-start(f32[1024,512]{1,0:T(8,128)S(1)} %convolution_dynamic-update-slice_fusion), channel_id=1, source_target_pairs={{0,1},{1,0},{2,3},{3,2},{4,5},{5,4},{6,7},{7,6},{8,9},{9,8},{10,11... | collective-permute-start | bytes 6291464 | tf_op jit(solution)/shard_map/ppermute | solution.py:21
  196.0 18.9 %collective-permute-start.49 = (bf16[128,1024]{1,0:T(8,128)(2,1)S(1)}, bf16[128,1024]{1,0:T(8,128)(2,1)S(1)}, u32[]{:S(2)}, u32[]{:S(2)}) collective-permute-start(bf16[128,1024]{1,0:T(8,128)(2,1)S(1)} %pad_maximum_fusion.7), channel_id=1, source_target_pairs={{0,2},{2,4},{4,6},{6,0},{1,3},{3,5},{5,7},{7,1},{8,10},{10,12},{12... | collective-permute-start | bytes 786440 | tf_op jit(solution)/shard_map/ppermute | solution.py:23
  196.9 18.0 %collective-permute-start.50 = (bf16[128,1024]{1,0:T(8,128)(2,1)S(1)}, bf16[128,1024]{1,0:T(8,128)(2,1)S(1)}, u32[]{:S(2)}, u32[]{:S(2)}) collective-permute-start(bf16[128,1024]{1,0:T(8,128)(2,1)S(1)} %pad_maximum_fusion.8), channel_id=1, source_target_pairs={{0,6},{2,0},{4,2},{6,4},{1,7},{3,1},{5,3},{7,5},{8,14},{10,8},{12,... | collective-permute-start | bytes 786440 | tf_op jit(solution)/shard_map/ppermute | solution.py:23
  199.5 15.5 %collective-permute-start.51 = (bf16[128,1024]{1,0:T(8,128)(2,1)S(1)}, bf16[128,1024]{1,0:T(8,128)(2,1)S(1)}, u32[]{:S(2)}, u32[]{:S(2)}) collective-permute-start(bf16[128,1024]{1,0:T(8,128)(2,1)S(1)} %pad_maximum_fusion.9), channel_id=1, source_target_pairs={{0,4},{2,6},{4,0},{6,2},{1,5},{3,7},{5,1},{7,3},{8,12},{10,14},{12... | collective-permute-start | bytes 786440 | tf_op jit(solution)/shard_map/ppermute | solution.py:23
  (28 other events, 219.9 us)
where the time goes:
time: 217 us; the launch traced here: 216 us
  waiting for transfers between devices  107 us (49%)
  starting transfers between devices  52.4 us (24%)
  Pallas kernels  27.4 us (13%)
  matrix products  24.1 us (11%)
  local copies, waits for them, and re-layouts  2.69 us (1%)
    ppermute x30, waiting for transfers between devices, send(): return lax.ppermute(values, ('row', 'depth'), perm)  97.8 us
    ppermute x30, starting transfers between devices, send(): return lax.ppermute(values, ('row', 'depth'), perm)  36 us
    ppermute x9, starting transfers between devices, send(): lax.ppermute(values, 'col', [(z, (z + shift) % SIDE) for z in range(SIDE)])  13.9 us
    dot_general x13, matrix products, back_product(): lax.dot_general(p, weights, (((1,), (1,)), ((), ())), preferred_element_t...  13.7 us
    pallas_call x2, Pallas kernels, weight_grads(): pl.pallas_call(functools.partial(grads_kernel, len(pieces), n_terms, bloc...  12.5 us
    dot_general x12, matrix products, partial(): return jnp.dot(tokens, weight, preferred_element_type=F32) * SCALE  10.4 us
    pallas_call x2, Pallas kernels, mask_weights(): pl.pallas_call(functools.partial(mask_kernel, rows // blocks, count), in_...  9.22 us
    ppermute x9, waiting for transfers between devices, send(): lax.ppermute(values, 'col', [(z, (z + shift) % SIDE) for z in range(SIDE)])  7.05 us
  transfers between devices with their start and end apart: 52, of which 21 were waited for; matrix products, arithmetic and copies ran while one was open for 12% of the time, Pallas kernels for 11%

commit v1 on v0

v1 whole, which is shorter than its diff:
```python
import functools

import jax
import jax.numpy as jnp
from jax import lax
from jax.experimental import pallas as pl
from jax.experimental.pallas import tpu as pltpu
from jax.sharding import PartitionSpec as P


BF16 = jnp.bfloat16
F16 = jnp.float16
F32 = jnp.float32
SIDE = 4
SCALE = 16.0
MIB = 1 << 20
WIDE = 256


def send(values, axis, shift):
    if axis == "core":
        return lax.ppermute(values, "depth", [(0, 1), (1, 0)])
    if axis == "z":
        return lax.ppermute(values, "col", [(z, (z + shift) % SIDE) for z in range(SIDE)])
    perm = []
    for y in range(SIDE):
        for x in range(SIDE):
            for core in range(2):
                along_x = (core == 0) == (axis == "first")
                to_y, to_x = (y, (x + shift) % SIDE) if along_x else ((y + shift) % SIDE, x)
                perm.append(((y * SIDE + x) * 2 + core, (to_y * SIDE + to_x) * 2 + core))
    return lax.ppermute(values, ("row", "depth"), perm)


def row_mask(mask, width, first, block):
    rows = lax.broadcasted_iota(jnp.int32, (mask.shape[1], width), 0)
    cols = lax.broadcasted_iota(jnp.int32, (mask.shape[1], width), 1) + first
    spread = jnp.logical_and(cols >= rows * block, cols < (rows + 1) * block).astype(F32)
    return jnp.dot(mask.astype(F32), spread, preferred_element_type=F32)


def mask_kernel(block, count, *refs):
    masks, weights, out = refs[:count], refs[count:-1], refs[-1]
    width = weights[0].shape[1]
    for j, (mask, weight) in enumerate(zip(masks, weights)):
        wide = row_mask(jnp.broadcast_to(mask[0], (8, mask.shape[2])), width, 0, block)
        out[:, pl.ds(j * width, width)] = (weight[...].astype(F32) * wide[0:1]).astype(BF16)


def mask_weights(weights, masks, vmem):
    rows, width = weights[0].shape
    count, (mrows, mcols) = len(weights), masks[0].shape
    block = rows // mrows
    return pl.pallas_call(
        functools.partial(mask_kernel, block, count),
        grid=(mrows,),
        in_specs=[pl.BlockSpec((1, 1, mcols), lambda i: (i, 0, 0))] * count
        + [pl.BlockSpec((block, width), lambda i: (i, 0))] * count,
        out_specs=pl.BlockSpec((block, count * width), lambda i: (i, 0)),
        out_shape=jax.ShapeDtypeStruct((rows, count * width), BF16),
        compiler_params=pltpu.CompilerParams(vmem_limit_bytes=vmem * MIB),
    )(*[m.reshape(mrows, 1, mcols) for m in masks], *weights)


def token_row(near, far):
    row, core = lax.axis_index("row"), lax.axis_index("depth")
    y, x = row // SIDE, lax.rem(row, SIDE)
    to_x = lax.rem(x + jnp.where(core == 0, near, far), SIDE)
    to_y = lax.rem(y + jnp.where(core == 0, far, near), SIDE)
    return pl.multiple_of((to_x * SIDE + to_y) * 8, 8)


def unroll_kernel(own, *refs):
    *got, out = refs
    total = own[...]
    for ref in got:
        total = total + ref[...].astype(F32)
    for i in range(16):
        out[pl.ds(token_row(i // SIDE, i % SIDE), 8), :] = total[i * 8:(i + 1) * 8]


def unroll_sum(own, got):
    whole = pl.BlockSpec(memory_space=pltpu.VMEM)
    return pl.pallas_call(
        unroll_kernel,
        in_specs=[whole] * (1 + len(got)),
        out_specs=whole,
        out_shape=jax.ShapeDtypeStruct(own.shape, F32),
        compiler_params=pltpu.CompilerParams(vmem_limit_bytes=4 * MIB),
        name="unroll_sum",
    )(own, *got)


def place_kernel(*refs):
    *pieces, out = refs
    slots = [(ref, at) for ref in pieces for at in range(0, ref.shape[0], 128)]

    @pl.loop(0, SIDE)
    def _(near):
        for far in range(SIDE):
            start = token_row(near, far)
            for i, (ref, at) in enumerate(slots):
                to = pl.multiple_of((near * SIDE + far) * 64 + i * 8, 8)
                out[pl.ds(to, 8), :] = ref[pl.ds(pl.multiple_of(at + start, 8), 8), :]


def place_tokens(pieces):
    whole = pl.BlockSpec(memory_space=pltpu.VMEM)
    rows = sum(p.shape[0] for p in pieces)
    return pl.pallas_call(
        place_kernel,
        in_specs=[whole] * len(pieces),
        out_specs=whole,
        out_shape=jax.ShapeDtypeStruct((rows, pieces[0].shape[1]), BF16),
        compiler_params=pltpu.CompilerParams(vmem_limit_bytes=6 * MIB),
    )(*pieces)


def join_kernel(*refs):
    *pieces, out, sems = refs
    copies = []
    for i, piece in enumerate(pieces):
        rows = piece.shape[0]
        copies.append(pltpu.make_async_copy(piece, out.at[pl.ds(i * rows, rows), :], sems.at[i]))
    for copy in copies:
        copy.start()
    for copy in copies:
        copy.wait()


def join_rows(pieces):
    return pl.pallas_call(
        join_kernel,
        in_specs=[pl.BlockSpec(memory_space=pl.ANY)] * len(pieces),
        out_specs=pl.BlockSpec(memory_space=pl.ANY),
        out_shape=jax.ShapeDtypeStruct((sum(p.shape[0] for p in pieces), pieces[0].shape[1]), BF16),
        scratch_shapes=[pltpu.SemaphoreType.DMA((len(pieces),))],
        compiler_params=pltpu.CompilerParams(vmem_limit_bytes=MIB),
    )(*pieces)


def masked_store(out, grad, mask, first, block):
    wide = row_mask(mask, out.shape[1], first, block)
    for i in range(mask.shape[0]):
        at = pl.ds(i * block, block)
        out[at, :] = grad[i * block:(i + 1) * block] * wide[i:i + 1]


def grads_kernel(n_pieces, n_terms, block, *refs):
    take = iter(refs)
    flipped = next(take)
    terms = [[next(take) for _ in range(n_pieces)] for _ in range(n_terms)]
    masks = [next(take) for _ in range(n_terms)]
    outs = [next(take) for _ in range(n_terms)]
    (joined,) = take
    step = pl.program_id(0)

    for pieces, mask, out in zip(terms, masks, outs):
        at = 0
        for piece in pieces:
            joined[pl.ds(at, piece.shape[0]), :] = piece[...]
            at += piece.shape[0]
        grad = jnp.dot(flipped[...], joined[...], preferred_element_type=F32)
        masked_store(out, grad, mask[...], step * out.shape[1], block)


def flip_kernel(tokens, out):
    @pl.loop(0, tokens.shape[0] // 128)
    def _(i):
        at = pl.ds(pl.multiple_of(i * 128, 128), 128)
        out[:, at] = tokens[at, :].T


def flip(tokens):
    return pl.pallas_call(
        flip_kernel,
        in_specs=[pl.BlockSpec(memory_space=pltpu.VMEM)],
        out_specs=pl.BlockSpec(memory_space=pltpu.VMEM),
        out_shape=jax.ShapeDtypeStruct(tokens.shape[::-1], tokens.dtype),
        compiler_params=pltpu.CompilerParams(vmem_limit_bytes=6 * MIB),
    )(tokens)


def weight_grads(flipped, terms, masks, wide=WIDE):
    features, total = flipped.shape
    n_terms, n_pieces = len(masks), len(terms[0])
    width = terms[0][0].shape[1]
    steps = width // wide
    whole = pl.BlockSpec(memory_space=pltpu.VMEM)
    block = features // masks[0].shape[0]
    out_spec = pl.BlockSpec((features, wide), lambda f: (0, f))
    return pl.pallas_call(
        functools.partial(grads_kernel, n_pieces, n_terms, block),
        grid=(steps,),
        in_specs=[whole]
        + [pl.BlockSpec((p.shape[0], wide), lambda f: (0, f)) for pieces in terms for p in pieces]
        + [whole] * n_terms,
        out_specs=[out_spec] * n_terms,
        out_shape=[jax.ShapeDtypeStruct((features, width), F32)] * n_terms,
        scratch_shapes=[pltpu.VMEM((total, wide), BF16)],
        compiler_params=pltpu.CompilerParams(vmem_limit_bytes=32 * MIB),
    )(flipped, *[p for pieces in terms for p in pieces], *masks)


def partial(tokens, weight):
    return jnp.dot(tokens, weight, preferred_element_type=F32) * SCALE


def sum_first(tokens, weight):
    from_left = send(partial(tokens[384:640], weight).astype(F16), "first", 1)
    from_right = send(partial(tokens[640:896], weight).astype(F16), "first", -1)
    low = (partial(tokens[256:384], weight) + from_left[128:].astype(F32)).astype(F16)
    low_left = send(low, "first", 1)
    high = (partial(tokens[896:], weight) + from_right[:128].astype(F32)).astype(F16)
    high_right = send(high, "first", -1)
    low = partial(tokens[:128], weight) + from_right[128:].astype(F32) + low_left.astype(F32)
    low = low.astype(F16)
    high = partial(tokens[128:256], weight) + from_left[:128].astype(F32) + high_right.astype(F32)
    high = high.astype(F16)
    return low, high


def sum_second(low, high):
    got = [send(values, "second", shift) for shift, values in ((1, low[64:]), (3, high[64:]), (2, high[:64]))]
    total = low[:64].astype(F32)
    for values in got:
        total = total + values.astype(F32)
    return total * (1.0 / SCALE)


def gather_second(values):
    got = {shift: send(values, "second", -shift) for shift in (1, 3, 2)}
    return [values, got[1], got[2], got[3]]


def gather_first(mine):
    left, right = send(mine, "first", 1), send(mine, "first", -1)
    far_low = send(left[:128], "first", 1)
    far_high = send(right[128:], "first", -1)
    return [mine, right, far_low, far_high, left]


def gather_first_two(one, two):
    one_left, two_right = send(one, "first", 1), send(two, "first", -1)
    two_left, one_right = send(two, "first", 1), send(one, "first", -1)
    one_far, two_far = send(one_left, "first", 1), send(two_right, "first", -1)
    return [one, one_right, one_far, one_left], [two, two_right, two_far, two_left]


def gather_tokens(own, joined):
    mine = {0: own}
    for shift in (1, 3, 2):
        mine[shift] = send(own, "z", -shift)
    pieces = [mine[i] for i in range(SIDE)]
    if joined:
        return place_tokens(pieces + [send(join_rows(pieces), "core", 1)])
    theirs = {shift: send(mine[shift], "core", 1) for shift in (0, 1, 3, 2)}
    return place_tokens(pieces + [theirs[i] for i in range(SIDE)])


def chip_kernel(sizes, *refs):
    count = len(sizes)
    mine, theirs, (own, *outs), (kept, came, sems) = refs[:count], refs[count:2 * count], refs[2 * count:-3], refs[-3:]
    copies = []
    at = 0
    for i, size in enumerate(sizes):
        to = pl.ds(at, size)
        copies.append(pltpu.make_async_copy(mine[i].at[:, 0], kept.at[to], sems.at[0, i]))
        copies.append(pltpu.make_async_copy(theirs[i].at[:, 1], came.at[to], sems.at[1, i]))
        at += size
    for copy in copies:
        copy.start()
    for copy in copies:
        copy.wait()

    @pl.loop(0, SIDE)
    def _(near):
        for far in range(SIDE):
            total = kept[near * SIDE + far] + came[far * SIDE + near]
            at = pl.ds(pl.multiple_of((near * SIDE + far) * 8, 8), 8)
            own[at, :] = total[:8]
            for z, out in enumerate(outs):
                out[at, :] = total[(z + 1) * 8:(z + 2) * 8].astype(BF16)


def chip_sum(mine, theirs):
    features = mine[0].shape[1]
    sizes = tuple(p.shape[0] // 64 for p in mine)
    shape = (sum(p.shape[0] for p in mine) // 8, features)
    whole = pl.BlockSpec(memory_space=pltpu.VMEM)
    return pl.pallas_call(
        functools.partial(chip_kernel, sizes),
        in_specs=[pl.BlockSpec(memory_space=pl.ANY)] * (2 * len(sizes)),
        out_specs=[whole] * SIDE,
        out_shape=[jax.ShapeDtypeStruct(shape, F32)] + [jax.ShapeDtypeStruct(shape, BF16)] * (SIDE - 1),
        scratch_shapes=[pltpu.VMEM((16, 32, features), F32)] * 2 + [pltpu.SemaphoreType.DMA((2, len(sizes)))],
        compiler_params=pltpu.CompilerParams(vmem_limit_bytes=6 * MIB),
        name="chip_sum",
    )(*[p.reshape(-1, 2, 32, features) for p in (*mine, *theirs)])


def back_product(groups):
    mine, theirs = [], []
    for pieces in groups:
        parts = [
            sum(lax.dot_general(t, w, (((1,), (1,)), ((), ())), preferred_element_type=F32) for t, w in pairs)
            for pairs in pieces
        ]
        mine.append(jnp.concatenate(parts, axis=0))
        theirs.append(send(mine[-1], "core", 1))
    own, *parts = chip_sum(mine, theirs)
    got = [send(parts[z - 1], "z", z) for z in (1, 3, 2)]
    return unroll_sum(own, got)


def per_device(
    tokens, out_grad, gate_weight, up_weight, down_weight, gate_mask, up_mask, down_mask
):
    w_gate_up = mask_weights((gate_weight, up_weight), (gate_mask, up_mask), 8)
    w_down = mask_weights((down_weight,), (down_mask,), 8)
    width = w_down.shape[1]

    ins = gather_tokens(tokens, False)
    outs = gather_tokens(out_grad, True)
    near_gate_up = sum_first(ins, w_gate_up)
    near_grad = sum_first(outs, w_down)

    gate_up = sum_second(*near_gate_up)
    gate, up = gate_up[:, :width], gate_up[:, width:]
    hidden = gather_second((gate * jax.nn.sigmoid(gate) * up).astype(BF16))
    hidden = gather_first(jnp.concatenate(hidden, axis=0))

    grad = sum_second(*near_grad)
    gate, up, grad = lax.optimization_barrier((gate, up, grad))
    sig = jax.nn.sigmoid(gate)
    act = gate * sig
    gate_term = (grad * up * sig * (1.0 + gate * (1.0 - sig))).astype(BF16)
    up_term = (grad * act).astype(BF16)
    terms = gather_second(jnp.concatenate([gate_term, up_term], axis=1))
    terms = gather_first_two(
        jnp.concatenate([t[:, :width] for t in terms], axis=0), jnp.concatenate([t[:, width:] for t in terms], axis=0)
    )

    outs_flipped = flip(outs)
    ins_flipped = flip(ins)

    w_pair = w_gate_up[:, :width], w_gate_up[:, width:]
    output = back_product([[[(h, w_down)] for h in hidden]])
    (down_grad,) = weight_grads(outs_flipped, [hidden], [down_mask])
    in_grad = back_product([[list(zip(pair, w_pair))] for pair in zip(*terms)])
    gate_grad, up_grad = weight_grads(ins_flipped, terms, [gate_mask, up_mask])
    return (output, in_grad, gate_grad, up_grad, down_grad)


def solution(mesh):
    data, weight = P(("col", "depth"), "row"), P("row", ("col", "depth"))

    return jax.shard_map(
        per_device,
        mesh=mesh,
        in_specs=(data,) * 2 + (weight,) * 6,
        out_specs=(data,) * 2 + (weight,) * 3,
        check_vma=False,
    )
```

time: 217 us -> 233 us (1.074)
  waiting for transfers between devices: 107 us -> 123 us
  starting transfers between devices: 52.4 us -> 65.5 us
  matrix products: 24.1 us -> 17 us
  Pallas kernels: 27.4 us -> 20.8 us
    ppermute x30, starting transfers between devices: 36 us -> 48.1 us  [send(): return lax.ppermute(values, ('row', 'depth'), perm)]
    ppermute x30, waiting for transfers between devices: 97.8 us -> 108 us  [send(): return lax.ppermute(values, ('row', 'depth'), perm)]
    pallas_call x8 -> x9, Pallas kernels: 25.3 us -> 18.7 us  [the longest x2 12.4 us: weight_grads(): pl.pallas_call(functools.partial(grads_kernel, n_pieces, n_terms, block),...]
    ppermute x9 -> x12, waiting for transfers between devices: 7.05 us -> 13.3 us  [send(): lax.ppermute(values, 'col', [(z, (z + shift) % SIDE) for z in range(SIDE)])]
    dot_general x13, matrix products: 13.7 us -> 8.76 us  [back_product(): lax.dot_general(t, w, (((1,), (1,)), ((), ())), preferred_element_type=F32)]
    ppermute x9 -> x12, starting transfers between devices: 13.9 us -> 16.5 us  [send(): lax.ppermute(values, 'col', [(z, (z + shift) % SIDE) for z in range(SIDE)])]
  transfers between devices with their start and end apart: 52 -> 52, of which waited for: 21 -> 26; matrix products, arithmetic and copies ran while one was open for 12% -> 8% of each run, Pallas kernels for 11% -> 8%
where the time goes in v1:
time: 233 us
  waiting for transfers between devices  123 us (53%)
  starting transfers between devices  65.5 us (28%)
  Pallas kernels  20.8 us (9%)
  matrix products  17 us (7%)
  local copies, waits for them, and re-layouts  3.63 us (2%)
    ppermute x30, waiting for transfers between devices, send(): return lax.ppermute(values, ('row', 'depth'), perm)  108 us
    ppermute x30, starting transfers between devices, send(): return lax.ppermute(values, ('row', 'depth'), perm)  48.1 us
    ppermute x12, starting transfers between devices, send(): lax.ppermute(values, 'col', [(z, (z + shift) % SIDE) for z in range(SIDE)])  16.5 us
    ppermute x12, waiting for transfers between devices, send(): lax.ppermute(values, 'col', [(z, (z + shift) % SIDE) for z in range(SIDE)])  13.3 us
    pallas_call x2, Pallas kernels, weight_grads(): pl.pallas_call(functools.partial(grads_kernel, n_pieces, n_terms, block),...  12.4 us
    dot_general x13, matrix products, back_product(): lax.dot_general(t, w, (((1,), (1,)), ((), ())), preferred_element_type=F32)  8.76 us
    dot_general x12, matrix products, partial(): return jnp.dot(tokens, weight, preferred_element_type=F32) * SCALE  8.23 us
  transfers between devices with their start and end apart: 52, of which 26 were waited for; matrix products, arithmetic and copies ran while one was open for 8% of the time, Pallas kernels for 8%

profile of v1, /device:TPU:0, one launch (start us, length us, event | category | flops | bytes accessed | tf_op | source)
XLA Modules:
  0.0 232.7 jit_solution(8145293088360273548)
XLA Ops:
  0.6 4.2 %collective-permute-start.25 = (bf16[128,512]{1,0:T(8,128)(2,1)}, bf16[128,512]{1,0:T(8,128)(2,1)S(1)}, u32[]{:S(2)}, u32[]{:S(2)}) collective-permute-start(bf16[128,512]{1,0:T(8,128)(2,1)} %refs_0_.5), channel_id=1, source_target_pairs={{0,6},{2,0},{4,2},{6,4},{1,7},{3,1},{5,3},{7,5},{8,14},{10,8},{12,... | collective-permute-start | bytes 393224 | tf_op jit(solution)/shard_map/ppermute | solution.py:24
  6.1 4.6 %collective-permute-done.25.refs_1_ = bf16[128,512]{1,0:T(8,128)(2,1)S(1)} collective-permute-done((bf16[128,512]{1,0:T(8,128)(2,1)}, bf16[128,512]{1,0:T(8,128)(2,1)S(1)}, u32[]{:S(2)}, u32[]{:S(2)}) %collective-permute-start.25) | collective-permute-done | bytes 131104 | tf_op jit(solution)/shard_map/ppermute | solution.py:24
  10.7 2.2 collective-permute-done.26.refs_2_
  22.4 2.4 %collective-permute-done.1.refs_2_ = bf16[128,512]{1,0:T(8,128)(2,1)S(1)} collective-permute-done((bf16[128,512]{1,0:T(8,128)(2,1)}, bf16[128,512]{1,0:T(8,128)(2,1)S(1)}, u32[]{:S(2)}, u32[]{:S(2)}) %collective-permute-start.1) | collective-permute-done | bytes 131104 | tf_op jit(solution)/shard_map/ppermute | solution.py:24
  28.0 2.8 %collective-permute-start.29 = (f16[256,1792]{1,0:T(8,128)(2,1)S(1)}, f16[256,1792]{1,0:T(8,128)(2,1)S(1)}, u32[]{:S(2)}, u32[]{:S(2)}) collective-permute-start(f16[256,1792]{1,0:T(8,128)(2,1)S(1)} %fusion.12), channel_id=1, source_target_pairs={{0,24},{1,97},{8,0},{9,105},{16,8},{17,113},{24,16},{25,121},{32,5... | collective-permute-start | bytes 2752520 | tf_op jit(solution)/shard_map/ppermute | solution.py:32
  37.1 4.7 %collective-permute-done.29 = f16[256,1792]{1,0:T(8,128)(2,1)S(1)} collective-permute-done((f16[256,1792]{1,0:T(8,128)(2,1)S(1)}, f16[256,1792]{1,0:T(8,128)(2,1)S(1)}, u32[]{:S(2)}, u32[]{:S(2)}) %collective-permute-start.29) | collective-permute-done | bytes 917536 | tf_op jit(solution)/shard_map/ppermute | solution.py:32
  42.2 3.8 %collective-permute-start.33 = (f16[128,1792]{1,0:T(8,128)(2,1)S(1)}, f16[128,1792]{1,0:T(8,128)(2,1)S(1)}, u32[]{:S(2)}, u32[]{:S(2)}) collective-permute-start(f16[128,1792]{1,0:T(8,128)(2,1)S(1)} %fusion.21), channel_id=1, source_target_pairs={{0,24},{1,97},{8,0},{9,105},{16,8},{17,113},{24,16},{25,121},{32,5... | collective-permute-start | bytes 1376264 | tf_op jit(solution)/shard_map/ppermute | solution.py:32
  47.1 3.4 %collective-permute-done.30 = f16[256,1792]{1,0:T(8,128)(2,1)S(1)} collective-permute-done((f16[256,1792]{1,0:T(8,128)(2,1)S(1)}, f16[256,1792]{1,0:T(8,128)(2,1)S(1)}, u32[]{:S(2)}, u32[]{:S(2)}) %collective-permute-start.30) | collective-permute-done | bytes 917536 | tf_op jit(solution)/shard_map/ppermute | solution.py:32
  51.1 15.2 %collective-permute-done.33 = f16[128,1792]{1,0:T(8,128)(2,1)S(1)} collective-permute-done((f16[128,1792]{1,0:T(8,128)(2,1)S(1)}, f16[128,1792]{1,0:T(8,128)(2,1)S(1)}, u32[]{:S(2)}, u32[]{:S(2)}) %collective-permute-start.33) | collective-permute-done | bytes 458784 | tf_op jit(solution)/shard_map/ppermute | solution.py:32
  67.5 3.8 %collective-permute-start.11 = (f16[128,3584]{1,0:T(8,128)(2,1)S(1)}, f16[128,3584]{1,0:T(8,128)(2,1)S(1)}, u32[]{:S(2)}, u32[]{:S(2)}) collective-permute-start(f16[128,3584]{1,0:T(8,128)(2,1)S(1)} %fusion.11), channel_id=1, source_target_pairs={{0,24},{1,97},{8,0},{9,105},{16,8},{17,113},{24,16},{25,121},{32,5... | collective-permute-start | bytes 2752520 | tf_op jit(solution)/shard_map/ppermute | solution.py:32
  71.3 3.3 %collective-permute-start.35 = (f16[64,1792]{1,0:T(8,128)(2,1)S(1)}, f16[64,1792]{1,0:T(8,128)(2,1)S(1)}, u32[]{:S(2)}, u32[]{:S(2)}) collective-permute-start(f16[64,1792]{1,0:T(8,128)(2,1)S(1)} %get-tuple-element.45), channel_id=1, source_target_pairs={{0,64},{1,17},{8,72},{9,25},{16,80},{17,1},{24,88},{25,9},{32,96},... | collective-permute-start | bytes 688136 | tf_op jit(solution)/shard_map/ppermute | solution.py:32
  75.6 3.3 %collective-permute-done.31 = f16[128,1792]{1,0:T(8,128)(2,1)S(1)} collective-permute-done((f16[128,1792]{1,0:T(8,128)(2,1)S(1)}, f16[128,1792]{1,0:T(8,128)(2,1)S(1)}, u32[]{:S(2)}, u32[]{:S(2)}) %collective-permute-start.31) | collective-permute-done | bytes 458784 | tf_op jit(solution)/shard_map/ppermute | solution.py:32
  79.5 3.4 %collective-permute-start.32 = (f16[64,1792]{1,0:T(8,128)(2,1)S(1)}, f16[64,1792]{1,0:T(8,128)(2,1)S(1)}, u32[]{:S(2)}, u32[]{:S(2)}) collective-permute-start(f16[64,1792]{1,0:T(8,128)(2,1)S(1)} %slice.185), channel_id=1, source_target_pairs={{0,32},{1,9},{8,40},{9,17},{16,48},{17,25},{24,56},{25,1},{32,64},... | collective-permute-start | bytes 688136 | tf_op jit(solution)/shard_map/ppermute | solution.py:32
  83.6 3.4 %collective-permute-done.11 = f16[128,3584]{1,0:T(8,128)(2,1)S(1)} collective-permute-done((f16[128,3584]{1,0:T(8,128)(2,1)S(1)}, f16[128,3584]{1,0:T(8,128)(2,1)S(1)}, u32[]{:S(2)}, u32[]{:S(2)}) %collective-permute-start.11) | collective-permute-done | bytes 917536 | tf_op jit(solution)/shard_map/ppermute | solution.py:32
  88.0 2.1 collective-permute-start.13
  90.1 13.1 %collective-permute-done.9 = f16[128,3584]{1,0:T(8,128)(2,1)S(1)} collective-permute-done((f16[128,3584]{1,0:T(8,128)(2,1)S(1)}, f16[128,3584]{1,0:T(8,128)(2,1)S(1)}, u32[]{:S(2)}, u32[]{:S(2)}) %collective-permute-start.9) | collective-permute-done | bytes 917536 | tf_op jit(solution)/shard_map/ppermute | solution.py:32
  104.2 6.0 %collective-permute-start.10 = (f16[64,3584]{1,0:T(8,128)(2,1)S(1)}, f16[64,3584]{1,0:T(8,128)(2,1)S(1)}, u32[]{:S(2)}, u32[]{:S(2)}) collective-permute-start(f16[64,3584]{1,0:T(8,128)(2,1)S(1)} %slice.167), channel_id=1, source_target_pairs={{0,32},{1,9},{8,40},{9,17},{16,48},{17,25},{24,56},{25,1},{32,64},... | collective-permute-start | bytes 1376264 | tf_op jit(solution)/shard_map/ppermute | solution.py:32
  110.4 5.4 %collective-permute-done.12 = f16[64,3584]{1,0:T(8,128)(2,1)S(1)} collective-permute-done((f16[64,3584]{1,0:T(8,128)(2,1)S(1)}, f16[64,3584]{1,0:T(8,128)(2,1)S(1)}, u32[]{:S(2)}, u32[]{:S(2)}) %collective-permute-start.12) | collective-permute-done | bytes 458784 | tf_op jit(solution)/shard_map/ppermute | solution.py:32
  119.3 2.3 %collective-permute-start.15 = (bf16[64,1792]{1,0:T(8,128)(2,1)S(1)}, bf16[64,1792]{1,0:T(8,128)(2,1)S(1)}, u32[]{:S(2)}, u32[]{:S(2)}) collective-permute-start(bf16[64,1792]{1,0:T(8,128)(2,1)S(1)} %get-tuple-element.34), channel_id=1, source_target_pairs={{0,64},{1,17},{8,72},{9,25},{16,80},{17,1},{24,88},{25,9},{32,96},... | collective-permute-start | bytes 688136 | tf_op jit(solution)/shard_map/ppermute | solution.py:32
  121.6 2.4 %collective-permute-start.14 = (bf16[64,1792]{1,0:T(8,128)(2,1)S(1)}, bf16[64,1792]{1,0:T(8,128)(2,1)S(1)}, u32[]{:S(2)}, u32[]{:S(2)}) collective-permute-start(bf16[64,1792]{1,0:T(8,128)(2,1)S(1)} %get-tuple-element.34), channel_id=1, source_target_pairs={{0,96},{1,25},{8,104},{9,1},{16,112},{17,9},{24,120},{25,17},{32,0... | collective-permute-start | bytes 688136 | tf_op jit(solution)/shard_map/ppermute | solution.py:32
  128.6 4.4 %collective-permute-done.15 = bf16[64,1792]{1,0:T(8,128)(2,1)S(1)} collective-permute-done((bf16[64,1792]{1,0:T(8,128)(2,1)S(1)}, bf16[64,1792]{1,0:T(8,128)(2,1)S(1)}, u32[]{:S(2)}, u32[]{:S(2)}) %collective-permute-start.15) | collective-permute-done | bytes 229408 | tf_op jit(solution)/shard_map/ppermute | solution.py:32
  136.4 4.4 %collective-permute-done.38 = bf16[64,3584]{1,0:T(8,128)(2,1)S(1)} collective-permute-done((bf16[64,3584]{1,0:T(8,128)(2,1)S(1)}, bf16[64,3584]{1,0:T(8,128)(2,1)S(1)}, u32[]{:S(2)}, u32[]{:S(2)}) %collective-permute-start.38) | collective-permute-done | bytes 458784 | tf_op jit(solution)/shard_map/ppermute | solution.py:32
  140.9 11.7 %collective-permute-done.37 = bf16[64,3584]{1,0:T(8,128)(2,1)S(1)} collective-permute-done((bf16[64,3584]{1,0:T(8,128)(2,1)S(1)}, bf16[64,3584]{1,0:T(8,128)(2,1)S(1)}, u32[]{:S(2)}, u32[]{:S(2)}) %collective-permute-start.37) | collective-permute-done | bytes 458784 | tf_op jit(solution)/shard_map/ppermute | solution.py:32
  159.9 16.8 %collective-permute-done.40.refs_6_ = bf16[256,1792]{1,0:T(8,128)(2,1)S(1)} collective-permute-done((bf16[256,1792]{1,0:T(8,128)(2,1)S(1)}, bf16[256,1792]{1,0:T(8,128)(2,1)S(1)}, u32[]{:S(2)}, u32[]{:S(2)}) %collective-permute-start.40) | collective-permute-done | bytes 917536 | tf_op jit(solution)/shard_map/ppermute | solution.py:32
  178.5 4.3 %collective-permute-done.19.refs_3_ = bf16[128,1792]{1,0:T(8,128)(2,1)S(1)} collective-permute-done((bf16[128,1792]{1,0:T(8,128)(2,1)S(1)}, bf16[128,1792]{1,0:T(8,128)(2,1)S(1)}, u32[]{:S(2)}, u32[]{:S(2)}) %collective-permute-start.19) | collective-permute-done | bytes 458784 | tf_op jit(solution)/shard_map/ppermute | solution.py:32
  185.1 2.4 %collective-permute-start.43 = (bf16[256,1792]{1,0:T(8,128)(2,1)S(1)}, bf16[256,1792]{1,0:T(8,128)(2,1)S(1)}, u32[]{:S(2)}, u32[]{:S(2)}) collective-permute-start(bf16[256,1792]{1,0:T(8,128)(2,1)S(1)} %collective-permute-done.40.refs_6_), channel_id=1, source_target_pairs={{0,24},{1,97},{8,0},{9,105},{16,8},{17,113},{24,16},{25,121},{32,5... | collective-permute-start | bytes 2752520 | tf_op jit(solution)/shard_map/ppermute | solution.py:32
  191.7 6.8 %collective-permute-done.43.refs_7_ = bf16[256,1792]{1,0:T(8,128)(2,1)S(1)} collective-permute-done((bf16[256,1792]{1,0:T(8,128)(2,1)S(1)}, bf16[256,1792]{1,0:T(8,128)(2,1)S(1)}, u32[]{:S(2)}, u32[]{:S(2)}) %collective-permute-start.43) | collective-permute-done | bytes 917536 | tf_op jit(solution)/shard_map/ppermute | solution.py:32
  199.2 5.7 %collective-permute-done.42.refs_3_ = bf16[256,1792]{1,0:T(8,128)(2,1)S(1)} collective-permute-done((bf16[256,1792]{1,0:T(8,128)(2,1)S(1)}, bf16[256,1792]{1,0:T(8,128)(2,1)S(1)}, u32[]{:S(2)}, u32[]{:S(2)}) %collective-permute-start.42) | collective-permute-done | bytes 917536 | tf_op jit(solution)/shard_map/ppermute | solution.py:32
  208.0 3.2 %collective-permute-start.50 = (bf16[128,512]{1,0:T(8,128)(2,1)S(1)}, bf16[128,512]{1,0:T(8,128)(2,1)S(1)}, u32[]{:S(2)}, u32[]{:S(2)}) collective-permute-start(bf16[128,512]{1,0:T(8,128)(2,1)S(1)} %get-tuple-element.27), channel_id=1, source_target_pairs={{0,6},{2,0},{4,2},{6,4},{1,7},{3,1},{5,3},{7,5},{8,14},{10,8},{12,... | collective-permute-start | bytes 393224 | tf_op jit(solution)/shard_map/ppermute | solution.py:24
  214.8 2.3 collective-permute-start.24
  218.7 5.3 %shard_map.127 = f32[512,1792]{1,0:T(8,128)} custom-call(bf16[512,1024]{1,0:T(8,128)(2,1)S(1)} %shard_map.126.refs_0_, bf16[256,1792]{1,0:T(8,128)(2,1)S(1)} %pad_maximum_fusion.refs_1_, bf16[256,1792]{1,0:T(8,128)(2,1)S(1)} %collective-permute-done.17.refs_2_, bf16[128,1792]{1,0:T(8,128)(2,1)S(1)} %collective-permute-done.19.refs_3_, ...), custom_call_target="tpu_custom_call" | custom-call | tf_op jit(solution)/shard_map/pallas_call | solution.py:192
  224.0 7.1 %shard_map.125 = (f32[512,1792]{1,0:T(8,128)}, f32[512,1792]{1,0:T(8,128)}) custom-call(bf16[512,1024]{1,0:T(8,128)(2,1)S(1)} %shard_map.124.refs_0_, bf16[256,1792]{1,0:T(8,128)(2,1)S(1)} %pad_maximum_fusion.1.refs_1_, bf16[256,1792]{1,0:T(8,128)(2,1)S(1)} %collective-permute-done.39.refs_2_, bf16[256,1792]{1,0:T(8,128)(2,1)S(1)} %collective-permute-done.42.refs_3_, ...), custom_call_target="tpu_custom_call" | custom-call | tf_op jit(solution)/shard_map/pallas_call | solution.py:192
  (147 shorter events, 65.2 us)
Async XLA Ops:
  17.8 14.8 %collective-permute-start.3 = (bf16[128,512]{1,0:T(8,128)(2,1)}, bf16[128,512]{1,0:T(8,128)(2,1)S(1)}, u32[]{:S(2)}, u32[]{:S(2)}) collective-permute-start(bf16[128,512]{1,0:T(8,128)(2,1)} %refs_0_.3), channel_id=1, source_target_pairs={{0,1},{1,0},{2,3},{3,2},{4,5},{5,4},{6,7},{7,6},{8,9},{9,8},{10,11... | collective-permute-start | bytes 393224 | tf_op jit(solution)/shard_map/ppermute | solution.py:22
  28.0 13.7 %collective-permute-start.29 = (f16[256,1792]{1,0:T(8,128)(2,1)S(1)}, f16[256,1792]{1,0:T(8,128)(2,1)S(1)}, u32[]{:S(2)}, u32[]{:S(2)}) collective-permute-start(f16[256,1792]{1,0:T(8,128)(2,1)S(1)} %fusion.12), channel_id=1, source_target_pairs={{0,24},{1,97},{8,0},{9,105},{16,8},{17,113},{24,16},{25,121},{32,5... | collective-permute-start | bytes 2752520 | tf_op jit(solution)/shard_map/ppermute | solution.py:32
  34.3 32.5 %collective-permute-start.7 = (f16[256,3584]{1,0:T(8,128)(2,1)S(1)}, f16[256,3584]{1,0:T(8,128)(2,1)S(1)}, u32[]{:S(2)}, u32[]{:S(2)}) collective-permute-start(f16[256,3584]{1,0:T(8,128)(2,1)S(1)} %fusion), channel_id=1, source_target_pairs={{0,24},{1,97},{8,0},{9,105},{16,8},{17,113},{24,16},{25,121},{32,5... | collective-permute-start | bytes 5505032 | tf_op jit(solution)/shard_map/ppermute | solution.py:32
  35.9 14.7 %collective-permute-start.30 = (f16[256,1792]{1,0:T(8,128)(2,1)S(1)}, f16[256,1792]{1,0:T(8,128)(2,1)S(1)}, u32[]{:S(2)}, u32[]{:S(2)}) collective-permute-start(f16[256,1792]{1,0:T(8,128)(2,1)S(1)} %fusion.13), channel_id=1, source_target_pairs={{0,8},{1,33},{8,16},{9,41},{16,24},{17,49},{24,0},{25,57},{32,40},... | collective-permute-start | bytes 2752520 | tf_op jit(solution)/shard_map/ppermute | solution.py:32
  42.2 24.1 %collective-permute-start.33 = (f16[128,1792]{1,0:T(8,128)(2,1)S(1)}, f16[128,1792]{1,0:T(8,128)(2,1)S(1)}, u32[]{:S(2)}, u32[]{:S(2)}) collective-permute-start(f16[128,1792]{1,0:T(8,128)(2,1)S(1)} %fusion.21), channel_id=1, source_target_pairs={{0,24},{1,97},{8,0},{9,105},{16,8},{17,113},{24,16},{25,121},{32,5... | collective-permute-start | bytes 1376264 | tf_op jit(solution)/shard_map/ppermute | solution.py:32
  47.1 35.8 %collective-permute-start.8 = (f16[256,3584]{1,0:T(8,128)(2,1)S(1)}, f16[256,3584]{1,0:T(8,128)(2,1)S(1)}, u32[]{:S(2)}, u32[]{:S(2)}) collective-permute-start(f16[256,3584]{1,0:T(8,128)(2,1)S(1)} %fusion.1), channel_id=1, source_target_pairs={{0,8},{1,33},{8,16},{9,41},{16,24},{17,49},{24,0},{25,57},{32,40},... | collective-permute-start | bytes 5505032 | tf_op jit(solution)/shard_map/ppermute | solution.py:32
  51.0 27.9 %collective-permute-start.31 = (f16[128,1792]{1,0:T(8,128)(2,1)S(1)}, f16[128,1792]{1,0:T(8,128)(2,1)S(1)}, u32[]{:S(2)}, u32[]{:S(2)}) collective-permute-start(f16[128,1792]{1,0:T(8,128)(2,1)S(1)} %fusion.20), channel_id=1, source_target_pairs={{0,8},{1,33},{8,16},{9,41},{16,24},{17,49},{24,0},{25,57},{32,40},... | collective-permute-start | bytes 1376264 | tf_op jit(solution)/shard_map/ppermute | solution.py:32
  67.5 19.6 %collective-permute-start.11 = (f16[128,3584]{1,0:T(8,128)(2,1)S(1)}, f16[128,3584]{1,0:T(8,128)(2,1)S(1)}, u32[]{:S(2)}, u32[]{:S(2)}) collective-permute-start(f16[128,3584]{1,0:T(8,128)(2,1)S(1)} %fusion.11), channel_id=1, source_target_pairs={{0,24},{1,97},{8,0},{9,105},{16,8},{17,113},{24,16},{25,121},{32,5... | collective-permute-start | bytes 2752520 | tf_op jit(solution)/shard_map/ppermute | solution.py:32
  71.3 32.9 %collective-permute-start.35 = (f16[64,1792]{1,0:T(8,128)(2,1)S(1)}, f16[64,1792]{1,0:T(8,128)(2,1)S(1)}, u32[]{:S(2)}, u32[]{:S(2)}) collective-permute-start(f16[64,1792]{1,0:T(8,128)(2,1)S(1)} %get-tuple-element.45), channel_id=1, source_target_pairs={{0,64},{1,17},{8,72},{9,25},{16,80},{17,1},{24,88},{25,9},{32,96},... | collective-permute-start | bytes 688136 | tf_op jit(solution)/shard_map/ppermute | solution.py:32
  74.6 35.6 %collective-permute-start.34 = (f16[64,1792]{1,0:T(8,128)(2,1)S(1)}, f16[64,1792]{1,0:T(8,128)(2,1)S(1)}, u32[]{:S(2)}, u32[]{:S(2)}) collective-permute-start(f16[64,1792]{1,0:T(8,128)(2,1)S(1)} %get-tuple-element.44), channel_id=1, source_target_pairs={{0,96},{1,25},{8,104},{9,1},{16,112},{17,9},{24,120},{25,17},{32,0... | collective-permute-start | bytes 688136 | tf_op jit(solution)/shard_map/ppermute | solution.py:32
  79.5 30.8 %collective-permute-start.32 = (f16[64,1792]{1,0:T(8,128)(2,1)S(1)}, f16[64,1792]{1,0:T(8,128)(2,1)S(1)}, u32[]{:S(2)}, u32[]{:S(2)}) collective-permute-start(f16[64,1792]{1,0:T(8,128)(2,1)S(1)} %slice.185), channel_id=1, source_target_pairs={{0,32},{1,9},{8,40},{9,17},{16,48},{17,25},{24,56},{25,1},{32,64},... | collective-permute-start | bytes 688136 | tf_op jit(solution)/shard_map/ppermute | solution.py:32
  83.6 19.6 %collective-permute-start.9 = (f16[128,3584]{1,0:T(8,128)(2,1)S(1)}, f16[128,3584]{1,0:T(8,128)(2,1)S(1)}, u32[]{:S(2)}, u32[]{:S(2)}) collective-permute-start(f16[128,3584]{1,0:T(8,128)(2,1)S(1)} %fusion.9), channel_id=1, source_target_pairs={{0,8},{1,33},{8,16},{9,41},{16,24},{17,49},{24,0},{25,57},{32,40},... | collective-permute-start | bytes 2752520 | tf_op jit(solution)/shard_map/ppermute | solution.py:32
  88.0 22.3 %collective-permute-start.13 = (f16[64,3584]{1,0:T(8,128)(2,1)S(1)}, f16[64,3584]{1,0:T(8,128)(2,1)S(1)}, u32[]{:S(2)}, u32[]{:S(2)}) collective-permute-start(f16[64,3584]{1,0:T(8,128)(2,1)S(1)} %get-tuple-element.37), channel_id=1, source_target_pairs={{0,64},{1,17},{8,72},{9,25},{16,80},{17,1},{24,88},{25,9},{32,96},... | collective-permute-start | bytes 1376264 | tf_op jit(solution)/shard_map/ppermute | solution.py:32
  124.3 16.6 %collective-permute-start.38 = (bf16[64,3584]{1,0:T(8,128)(2,1)S(1)}, bf16[64,3584]{1,0:T(8,128)(2,1)S(1)}, u32[]{:S(2)}, u32[]{:S(2)}) collective-permute-start(bf16[64,3584]{1,0:T(8,128)(2,1)S(1)} %pad_maximum_fusion.3), channel_id=1, source_target_pairs={{0,32},{1,9},{8,40},{9,17},{16,48},{17,25},{24,56},{25,1},{32,64},... | collective-permute-start | bytes 1376264 | tf_op jit(solution)/shard_map/ppermute | solution.py:32
  124.3 28.3 %collective-permute-start.37 = (bf16[64,3584]{1,0:T(8,128)(2,1)S(1)}, bf16[64,3584]{1,0:T(8,128)(2,1)S(1)}, u32[]{:S(2)}, u32[]{:S(2)}) collective-permute-start(bf16[64,3584]{1,0:T(8,128)(2,1)S(1)} %pad_maximum_fusion.3), channel_id=1, source_target_pairs={{0,64},{1,17},{8,72},{9,25},{16,80},{17,1},{24,88},{25,9},{32,96},... | collective-permute-start | bytes 1376264 | tf_op jit(solution)/shard_map/ppermute | solution.py:32
  126.7 26.5 %collective-permute-start.36 = (bf16[64,3584]{1,0:T(8,128)(2,1)S(1)}, bf16[64,3584]{1,0:T(8,128)(2,1)S(1)}, u32[]{:S(2)}, u32[]{:S(2)}) collective-permute-start(bf16[64,3584]{1,0:T(8,128)(2,1)S(1)} %pad_maximum_fusion.3), channel_id=1, source_target_pairs={{0,96},{1,25},{8,104},{9,1},{16,112},{17,9},{24,120},{25,17},{32,0... | collective-permute-start | bytes 1376264 | tf_op jit(solution)/shard_map/ppermute | solution.py:32
  133.7 25.4 %collective-permute-start.17 = (bf16[256,1792]{1,0:T(8,128)(2,1)S(1)}, bf16[256,1792]{1,0:T(8,128)(2,1)S(1)}, u32[]{:S(2)}, u32[]{:S(2)}) collective-permute-start(bf16[256,1792]{1,0:T(8,128)(2,1)S(1)} %pad_maximum_fusion.refs_1_), channel_id=1, source_target_pairs={{0,24},{1,97},{8,0},{9,105},{16,8},{17,113},{24,16},{25,121},{32,5... | collective-permute-start | bytes 2752520 | tf_op jit(solution)/shard_map/ppermute | solution.py:32
  133.7 24.5 %collective-permute-start.18 = (bf16[256,1792]{1,0:T(8,128)(2,1)S(1)}, bf16[256,1792]{1,0:T(8,128)(2,1)S(1)}, u32[]{:S(2)}, u32[]{:S(2)}) collective-permute-start(bf16[256,1792]{1,0:T(8,128)(2,1)S(1)} %pad_maximum_fusion.refs_1_), channel_id=1, source_target_pairs={{0,8},{1,33},{8,16},{9,41},{16,24},{17,49},{24,0},{25,57},{32,40},... | collective-permute-start | bytes 2752520 | tf_op jit(solution)/shard_map/ppermute | solution.py:32
  153.4 35.6 %collective-permute-start.39 = (bf16[256,1792]{1,0:T(8,128)(2,1)S(1)}, bf16[256,1792]{1,0:T(8,128)(2,1)S(1)}, u32[]{:S(2)}, u32[]{:S(2)}) collective-permute-start(bf16[256,1792]{1,0:T(8,128)(2,1)S(1)} %pad_maximum_fusion.1.refs_1_), channel_id=1, source_target_pairs={{0,24},{1,97},{8,0},{9,105},{16,8},{17,113},{24,16},{25,121},{32,5... | collective-permute-start | bytes 2752520 | tf_op jit(solution)/shard_map/ppermute | solution.py:32
  153.4 36.3 %collective-permute-start.41 = (bf16[256,1792]{1,0:T(8,128)(2,1)S(1)}, bf16[256,1792]{1,0:T(8,128)(2,1)S(1)}, u32[]{:S(2)}, u32[]{:S(2)}) collective-permute-start(bf16[256,1792]{1,0:T(8,128)(2,1)S(1)} %pad_maximum_fusion.1.refs_1_), channel_id=1, source_target_pairs={{0,8},{1,33},{8,16},{9,41},{16,24},{17,49},{24,0},{25,57},{32,40},... | collective-permute-start | bytes 2752520 | tf_op jit(solution)/shard_map/ppermute | solution.py:32
  155.5 21.1 %collective-permute-start.40 = (bf16[256,1792]{1,0:T(8,128)(2,1)S(1)}, bf16[256,1792]{1,0:T(8,128)(2,1)S(1)}, u32[]{:S(2)}, u32[]{:S(2)}) collective-permute-start(bf16[256,1792]{1,0:T(8,128)(2,1)S(1)} %pad_maximum_fusion.2.refs_5_), channel_id=1, source_target_pairs={{0,24},{1,97},{8,0},{9,105},{16,8},{17,113},{24,16},{25,121},{32,5... | collective-permute-start | bytes 2752520 | tf_op jit(solution)/shard_map/ppermute | solution.py:32
  158.2 32.1 %collective-permute-start.44 = (bf16[256,1792]{1,0:T(8,128)(2,1)S(1)}, bf16[256,1792]{1,0:T(8,128)(2,1)S(1)}, u32[]{:S(2)}, u32[]{:S(2)}) collective-permute-start(bf16[256,1792]{1,0:T(8,128)(2,1)S(1)} %pad_maximum_fusion.2.refs_5_), channel_id=1, source_target_pairs={{0,8},{1,33},{8,16},{9,41},{16,24},{17,49},{24,0},{25,57},{32,40},... | collective-permute-start | bytes 2752520 | tf_op jit(solution)/shard_map/ppermute | solution.py:32
  159.1 23.8 %collective-permute-start.19 = (bf16[128,1792]{1,0:T(8,128)(2,1)S(1)}, bf16[128,1792]{1,0:T(8,128)(2,1)S(1)}, u32[]{:S(2)}, u32[]{:S(2)}) collective-permute-start(bf16[128,1792]{1,0:T(8,128)(2,1)S(1)} %slice.176), channel_id=1, source_target_pairs={{0,8},{1,33},{8,16},{9,41},{16,24},{17,49},{24,0},{25,57},{32,40},... | collective-permute-start | bytes 1376264 | tf_op jit(solution)/shard_map/ppermute | solution.py:32
  182.9 22.8 %collective-permute-start.45 = (f32[256,512]{1,0:T(8,128)S(1)}, f32[256,512]{1,0:T(8,128)S(1)}, u32[]{:S(2)}, u32[]{:S(2)}) collective-permute-start(f32[256,512]{1,0:T(8,128)S(1)} %convolution_add_fusion.3), channel_id=1, source_target_pairs={{0,1},{1,0},{2,3},{3,2},{4,5},{5,4},{6,7},{7,6},{8,9},{9,8},{10,11... | collective-permute-start | bytes 1572872 | tf_op jit(solution)/shard_map/ppermute | solution.py:22
  189.0 22.3 %collective-permute-start.21 = (f32[1024,512]{1,0:T(8,128)S(1)}, f32[1024,512]{1,0:T(8,128)S(1)}, u32[]{:S(2)}, u32[]{:S(2)}) collective-permute-start(f32[1024,512]{1,0:T(8,128)S(1)} %convolution_dynamic-update-slice_fusion), channel_id=1, source_target_pairs={{0,1},{1,0},{2,3},{3,2},{4,5},{5,4},{6,7},{7,6},{8,9},{9,8},{10,11... | collective-permute-start | bytes 6291464 | tf_op jit(solution)/shard_map/ppermute | solution.py:22
  189.8 16.0 %collective-permute-start.46 = (f32[256,512]{1,0:T(8,128)S(1)}, f32[256,512]{1,0:T(8,128)S(1)}, u32[]{:S(2)}, u32[]{:S(2)}) collective-permute-start(f32[256,512]{1,0:T(8,128)S(1)} %convolution_add_fusion.2), channel_id=1, source_target_pairs={{0,1},{1,0},{2,3},{3,2},{4,5},{5,4},{6,7},{7,6},{8,9},{9,8},{10,11... | collective-permute-start | bytes 1572872 | tf_op jit(solution)/shard_map/ppermute | solution.py:22
  190.3 14.6 %collective-permute-start.42 = (bf16[256,1792]{1,0:T(8,128)(2,1)S(1)}, bf16[256,1792]{1,0:T(8,128)(2,1)S(1)}, u32[]{:S(2)}, u32[]{:S(2)}) collective-permute-start(bf16[256,1792]{1,0:T(8,128)(2,1)S(1)} %collective-permute-done.41.refs_4_), channel_id=1, source_target_pairs={{0,8},{1,33},{8,16},{9,41},{16,24},{17,49},{24,0},{25,57},{32,40},... | collective-permute-start | bytes 2752520 | tf_op jit(solution)/shard_map/ppermute | solution.py:32
  208.0 23.0 %collective-permute-start.50 = (bf16[128,512]{1,0:T(8,128)(2,1)S(1)}, bf16[128,512]{1,0:T(8,128)(2,1)S(1)}, u32[]{:S(2)}, u32[]{:S(2)}) collective-permute-start(bf16[128,512]{1,0:T(8,128)(2,1)S(1)} %get-tuple-element.27), channel_id=1, source_target_pairs={{0,6},{2,0},{4,2},{6,4},{1,7},{3,1},{5,3},{7,5},{8,14},{10,8},{12,... | collective-permute-start | bytes 393224 | tf_op jit(solution)/shard_map/ppermute | solution.py:24
  211.3 19.8 %collective-permute-start.51 = (bf16[128,512]{1,0:T(8,128)(2,1)S(1)}, bf16[128,512]{1,0:T(8,128)(2,1)S(1)}, u32[]{:S(2)}, u32[]{:S(2)}) collective-permute-start(bf16[128,512]{1,0:T(8,128)(2,1)S(1)} %get-tuple-element.28), channel_id=1, source_target_pairs={{0,4},{2,6},{4,0},{6,2},{1,5},{3,7},{5,1},{7,3},{8,12},{10,14},{12... | collective-permute-start | bytes 393224 | tf_op jit(solution)/shard_map/ppermute | solution.py:24
  211.5 20.3 %collective-permute-start.22 = (bf16[128,512]{1,0:T(8,128)(2,1)S(1)}, bf16[128,512]{1,0:T(8,128)(2,1)S(1)}, u32[]{:S(2)}, u32[]{:S(2)}) collective-permute-start(bf16[128,512]{1,0:T(8,128)(2,1)S(1)} %get-tuple-element.19), channel_id=1, source_target_pairs={{0,2},{2,4},{4,6},{6,0},{1,3},{3,5},{5,7},{7,1},{8,10},{10,12},{12... | collective-permute-start | bytes 393224 | tf_op jit(solution)/shard_map/ppermute | solution.py:24
  212.8 19.0 %collective-permute-start.23 = (bf16[128,512]{1,0:T(8,128)(2,1)S(1)}, bf16[128,512]{1,0:T(8,128)(2,1)S(1)}, u32[]{:S(2)}, u32[]{:S(2)}) collective-permute-start(bf16[128,512]{1,0:T(8,128)(2,1)S(1)} %get-tuple-element.20), channel_id=1, source_target_pairs={{0,6},{2,0},{4,2},{6,4},{1,7},{3,1},{5,3},{7,5},{8,14},{10,8},{12,... | collective-permute-start | bytes 393224 | tf_op jit(solution)/shard_map/ppermute | solution.py:24
  214.8 17.0 %collective-permute-start.24 = (bf16[128,512]{1,0:T(8,128)(2,1)S(1)}, bf16[128,512]{1,0:T(8,128)(2,1)S(1)}, u32[]{:S(2)}, u32[]{:S(2)}) collective-permute-start(bf16[128,512]{1,0:T(8,128)(2,1)S(1)} %get-tuple-element.21), channel_id=1, source_target_pairs={{0,4},{2,6},{4,0},{6,2},{1,5},{3,7},{5,1},{7,3},{8,12},{10,14},{12... | collective-permute-start | bytes 393224 | tf_op jit(solution)/shard_map/ppermute | solution.py:24
  (30 other events, 215.4 us)

commit v2 on v1

--- a/solution.py
+++ b/solution.py
@@ -60,6 +60,13 @@
         out_shape=jax.ShapeDtypeStruct((rows, count * width), BF16),
         compiler_params=pltpu.CompilerParams(vmem_limit_bytes=vmem * MIB),
     )(*[m.reshape(mrows, 1, mcols) for m in masks], *weights)
+
+
+def spread_mask(weight, mask):
+    (rows, width), (mrows, mcols) = weight.shape, mask.shape
+    pick = jnp.arange(width) // (width // mcols) == jnp.arange(mcols)[:, None]
+    wide = jnp.dot(mask.astype(BF16), pick.astype(BF16), preferred_element_type=F32).astype(BF16)
+    return (weight.reshape(mrows, rows // mrows, width) * wide[:, None, :]).reshape(rows, width)
 
 
 def token_row(near, far):
@@ -316,7 +323,9 @@
 def per_device(
     tokens, out_grad, gate_weight, up_weight, down_weight, gate_mask, up_mask, down_mask
 ):
-    w_gate_up = mask_weights((gate_weight, up_weight), (gate_mask, up_mask), 8)
+    w_gate_up = jnp.concatenate(
+        [spread_mask(gate_weight, gate_mask), spread_mask(up_weight, up_mask)], axis=1
+    )
     w_down = mask_weights((down_weight,), (down_mask,), 8)
     width = w_down.shape[1]
 
@@ -346,7 +355,7 @@
 
     w_pair = w_gate_up[:, :width], w_gate_up[:, width:]
     output = back_product([[[(h, w_down)] for h in hidden]])
-    (down_grad,) = weight_grads(outs_flipped, [hidden], [down_mask])
+    (down_grad,) = weight_grads(outs_flipped, [hidden], [down_mask], 896)
     in_grad = back_product([[list(zip(pair, w_pair))] for pair in zip(*terms)])
     gate_grad, up_grad = weight_grads(ins_flipped, terms, [gate_mask, up_mask])
     return (output, in_grad, gate_grad, up_grad, down_grad)

time: 233 us -> 232 us (level)
  Pallas kernels: 20.8 us -> 18.1 us
  transfers between devices with their start and end apart: 52 -> 52, of which waited for: 26 -> 26; matrix products, arithmetic and copies ran while one was open for 8% -> 8% of each run, Pallas kernels for 8% -> 7%
where the time goes in v2:
time: 232 us
  waiting for transfers between devices  124 us (53%)
  starting transfers between devices  65.7 us (28%)
  Pallas kernels  18.1 us (8%)
  matrix products  17.3 us (7%)
  local copies, waits for them, and re-layouts  4.19 us (2%)
    ppermute x30, waiting for transfers between devices, send(): return lax.ppermute(values, ('row', 'depth'), perm)  109 us
    ppermute x30, starting transfers between devices, send(): return lax.ppermute(values, ('row', 'depth'), perm)  48.4 us
    ppermute x12, starting transfers between devices, send(): lax.ppermute(values, 'col', [(z, (z + shift) % SIDE) for z in range(SIDE)])  16.5 us
    ppermute x12, waiting for transfers between devices, send(): lax.ppermute(values, 'col', [(z, (z + shift) % SIDE) for z in range(SIDE)])  13.1 us
    pallas_call x2, Pallas kernels, weight_grads(): pl.pallas_call(functools.partial(grads_kernel, n_pieces, n_terms, block),...  11.5 us
    dot_general x13, matrix products, back_product(): lax.dot_general(t, w, (((1,), (1,)), ((), ())), preferred_element_type=F32)  8.75 us
    dot_general x12, matrix products, partial(): return jnp.dot(tokens, weight, preferred_element_type=F32) * SCALE  8.25 us
  transfers between devices with their start and end apart: 52, of which 26 were waited for; matrix products, arithmetic and copies ran while one was open for 8% of the time, Pallas kernels for 7%

profile of v2, /device:TPU:0, one launch (start us, length us, event | category | flops | bytes accessed | tf_op | source)
XLA Modules:
  0.0 231.9 jit_solution(8274911746020007121)
XLA Ops:
  0.6 4.2 %collective-permute-start.25 = (bf16[128,512]{1,0:T(8,128)(2,1)}, bf16[128,512]{1,0:T(8,128)(2,1)S(1)}, u32[]{:S(2)}, u32[]{:S(2)}) collective-permute-start(bf16[128,512]{1,0:T(8,128)(2,1)} %refs_0_.5), channel_id=1, source_target_pairs={{0,6},{2,0},{4,2},{6,4},{1,7},{3,1},{5,3},{7,5},{8,14},{10,8},{12,... | collective-permute-start | bytes 393224 | tf_op jit(solution)/shard_map/ppermute | solution.py:24
  6.1 4.6 %collective-permute-done.25.refs_1_ = bf16[128,512]{1,0:T(8,128)(2,1)S(1)} collective-permute-done((bf16[128,512]{1,0:T(8,128)(2,1)}, bf16[128,512]{1,0:T(8,128)(2,1)S(1)}, u32[]{:S(2)}, u32[]{:S(2)}) %collective-permute-start.25) | collective-permute-done | bytes 131104 | tf_op jit(solution)/shard_map/ppermute | solution.py:24
  10.7 2.2 collective-permute-done.26.refs_2_
  22.4 2.4 %collective-permute-done.1.refs_2_ = bf16[128,512]{1,0:T(8,128)(2,1)S(1)} collective-permute-done((bf16[128,512]{1,0:T(8,128)(2,1)}, bf16[128,512]{1,0:T(8,128)(2,1)S(1)}, u32[]{:S(2)}, u32[]{:S(2)}) %collective-permute-start.1) | collective-permute-done | bytes 131104 | tf_op jit(solution)/shard_map/ppermute | solution.py:24
  28.0 2.8 %collective-permute-start.29 = (f16[256,1792]{1,0:T(8,128)(2,1)S(1)}, f16[256,1792]{1,0:T(8,128)(2,1)S(1)}, u32[]{:S(2)}, u32[]{:S(2)}) collective-permute-start(f16[256,1792]{1,0:T(8,128)(2,1)S(1)} %fusion.12), channel_id=1, source_target_pairs={{0,24},{1,97},{8,0},{9,105},{16,8},{17,113},{24,16},{25,121},{32,5... | collective-permute-start | bytes 2752520 | tf_op jit(solution)/shard_map/ppermute | solution.py:32
  36.2 5.5 %collective-permute-done.29 = f16[256,1792]{1,0:T(8,128)(2,1)S(1)} collective-permute-done((f16[256,1792]{1,0:T(8,128)(2,1)S(1)}, f16[256,1792]{1,0:T(8,128)(2,1)S(1)}, u32[]{:S(2)}, u32[]{:S(2)}) %collective-permute-start.29) | collective-permute-done | bytes 917536 | tf_op jit(solution)/shard_map/ppermute | solution.py:32
  42.2 3.8 %collective-permute-start.33 = (f16[128,1792]{1,0:T(8,128)(2,1)S(1)}, f16[128,1792]{1,0:T(8,128)(2,1)S(1)}, u32[]{:S(2)}, u32[]{:S(2)}) collective-permute-start(f16[128,1792]{1,0:T(8,128)(2,1)S(1)} %fusion.21), channel_id=1, source_target_pairs={{0,24},{1,97},{8,0},{9,105},{16,8},{17,113},{24,16},{25,121},{32,5... | collective-permute-start | bytes 1376264 | tf_op jit(solution)/shard_map/ppermute | solution.py:32
  47.1 2.5 %collective-permute-done.30 = f16[256,1792]{1,0:T(8,128)(2,1)S(1)} collective-permute-done((f16[256,1792]{1,0:T(8,128)(2,1)S(1)}, f16[256,1792]{1,0:T(8,128)(2,1)S(1)}, u32[]{:S(2)}, u32[]{:S(2)}) %collective-permute-start.30) | collective-permute-done | bytes 917536 | tf_op jit(solution)/shard_map/ppermute | solution.py:32
  50.1 16.2 %collective-permute-done.33 = f16[128,1792]{1,0:T(8,128)(2,1)S(1)} collective-permute-done((f16[128,1792]{1,0:T(8,128)(2,1)S(1)}, f16[128,1792]{1,0:T(8,128)(2,1)S(1)}, u32[]{:S(2)}, u32[]{:S(2)}) %collective-permute-start.33) | collective-permute-done | bytes 458784 | tf_op jit(solution)/shard_map/ppermute | solution.py:32
  67.5 3.8 %collective-permute-start.11 = (f16[128,3584]{1,0:T(8,128)(2,1)S(1)}, f16[128,3584]{1,0:T(8,128)(2,1)S(1)}, u32[]{:S(2)}, u32[]{:S(2)}) collective-permute-start(f16[128,3584]{1,0:T(8,128)(2,1)S(1)} %fusion.11), channel_id=1, source_target_pairs={{0,24},{1,97},{8,0},{9,105},{16,8},{17,113},{24,16},{25,121},{32,5... | collective-permute-start | bytes 2752520 | tf_op jit(solution)/shard_map/ppermute | solution.py:32
  71.3 3.5 %collective-permute-start.35 = (f16[64,1792]{1,0:T(8,128)(2,1)S(1)}, f16[64,1792]{1,0:T(8,128)(2,1)S(1)}, u32[]{:S(2)}, u32[]{:S(2)}) collective-permute-start(f16[64,1792]{1,0:T(8,128)(2,1)S(1)} %get-tuple-element.45), channel_id=1, source_target_pairs={{0,64},{1,17},{8,72},{9,25},{16,80},{17,1},{24,88},{25,9},{32,96},... | collective-permute-start | bytes 688136 | tf_op jit(solution)/shard_map/ppermute | solution.py:32
  75.8 3.1 %collective-permute-done.31 = f16[128,1792]{1,0:T(8,128)(2,1)S(1)} collective-permute-done((f16[128,1792]{1,0:T(8,128)(2,1)S(1)}, f16[128,1792]{1,0:T(8,128)(2,1)S(1)}, u32[]{:S(2)}, u32[]{:S(2)}) %collective-permute-start.31) | collective-permute-done | bytes 458784 | tf_op jit(solution)/shard_map/ppermute | solution.py:32
  79.4 3.5 %collective-permute-start.32 = (f16[64,1792]{1,0:T(8,128)(2,1)S(1)}, f16[64,1792]{1,0:T(8,128)(2,1)S(1)}, u32[]{:S(2)}, u32[]{:S(2)}) collective-permute-start(f16[64,1792]{1,0:T(8,128)(2,1)S(1)} %slice.177), channel_id=1, source_target_pairs={{0,32},{1,9},{8,40},{9,17},{16,48},{17,25},{24,56},{25,1},{32,64},... | collective-permute-start | bytes 688136 | tf_op jit(solution)/shard_map/ppermute | solution.py:32
  83.7 3.4 %collective-permute-done.11 = f16[128,3584]{1,0:T(8,128)(2,1)S(1)} collective-permute-done((f16[128,3584]{1,0:T(8,128)(2,1)S(1)}, f16[128,3584]{1,0:T(8,128)(2,1)S(1)}, u32[]{:S(2)}, u32[]{:S(2)}) %collective-permute-start.11) | collective-permute-done | bytes 917536 | tf_op jit(solution)/shard_map/ppermute | solution.py:32
  90.1 13.1 %collective-permute-done.9 = f16[128,3584]{1,0:T(8,128)(2,1)S(1)} collective-permute-done((f16[128,3584]{1,0:T(8,128)(2,1)S(1)}, f16[128,3584]{1,0:T(8,128)(2,1)S(1)}, u32[]{:S(2)}, u32[]{:S(2)}) %collective-permute-start.9) | collective-permute-done | bytes 917536 | tf_op jit(solution)/shard_map/ppermute | solution.py:32
  104.2 6.0 %collective-permute-start.10 = (f16[64,3584]{1,0:T(8,128)(2,1)S(1)}, f16[64,3584]{1,0:T(8,128)(2,1)S(1)}, u32[]{:S(2)}, u32[]{:S(2)}) collective-permute-start(f16[64,3584]{1,0:T(8,128)(2,1)S(1)} %slice.159), channel_id=1, source_target_pairs={{0,32},{1,9},{8,40},{9,17},{16,48},{17,25},{24,56},{25,1},{32,64},... | collective-permute-start | bytes 1376264 | tf_op jit(solution)/shard_map/ppermute | solution.py:32
  110.3 5.4 %collective-permute-done.12 = f16[64,3584]{1,0:T(8,128)(2,1)S(1)} collective-permute-done((f16[64,3584]{1,0:T(8,128)(2,1)S(1)}, f16[64,3584]{1,0:T(8,128)(2,1)S(1)}, u32[]{:S(2)}, u32[]{:S(2)}) %collective-permute-start.12) | collective-permute-done | bytes 458784 | tf_op jit(solution)/shard_map/ppermute | solution.py:32
  119.3 2.4 %collective-permute-start.15 = (bf16[64,1792]{1,0:T(8,128)(2,1)S(1)}, bf16[64,1792]{1,0:T(8,128)(2,1)S(1)}, u32[]{:S(2)}, u32[]{:S(2)}) collective-permute-start(bf16[64,1792]{1,0:T(8,128)(2,1)S(1)} %get-tuple-element.34), channel_id=1, source_target_pairs={{0,64},{1,17},{8,72},{9,25},{16,80},{17,1},{24,88},{25,9},{32,96},... | collective-permute-start | bytes 688136 | tf_op jit(solution)/shard_map/ppermute | solution.py:32
  121.7 2.3 collective-permute-start.14
  128.7 4.4 %collective-permute-done.15 = bf16[64,1792]{1,0:T(8,128)(2,1)S(1)} collective-permute-done((bf16[64,1792]{1,0:T(8,128)(2,1)S(1)}, bf16[64,1792]{1,0:T(8,128)(2,1)S(1)}, u32[]{:S(2)}, u32[]{:S(2)}) %collective-permute-start.15) | collective-permute-done | bytes 229408 | tf_op jit(solution)/shard_map/ppermute | solution.py:32
  136.5 4.4 %collective-permute-done.38 = bf16[64,3584]{1,0:T(8,128)(2,1)S(1)} collective-permute-done((bf16[64,3584]{1,0:T(8,128)(2,1)S(1)}, bf16[64,3584]{1,0:T(8,128)(2,1)S(1)}, u32[]{:S(2)}, u32[]{:S(2)}) %collective-permute-start.38) | collective-permute-done | bytes 458784 | tf_op jit(solution)/shard_map/ppermute | solution.py:32
  140.9 11.8 %collective-permute-done.37 = bf16[64,3584]{1,0:T(8,128)(2,1)S(1)} collective-permute-done((bf16[64,3584]{1,0:T(8,128)(2,1)S(1)}, bf16[64,3584]{1,0:T(8,128)(2,1)S(1)}, u32[]{:S(2)}, u32[]{:S(2)}) %collective-permute-start.37) | collective-permute-done | bytes 458784 | tf_op jit(solution)/shard_map/ppermute | solution.py:32
  160.2 16.5 %collective-permute-done.40.refs_6_ = bf16[256,1792]{1,0:T(8,128)(2,1)S(1)} collective-permute-done((bf16[256,1792]{1,0:T(8,128)(2,1)S(1)}, bf16[256,1792]{1,0:T(8,128)(2,1)S(1)}, u32[]{:S(2)}, u32[]{:S(2)}) %collective-permute-start.40) | collective-permute-done | bytes 917536 | tf_op jit(solution)/shard_map/ppermute | solution.py:32
  178.6 4.3 %collective-permute-done.19.refs_3_ = bf16[128,1792]{1,0:T(8,128)(2,1)S(1)} collective-permute-done((bf16[128,1792]{1,0:T(8,128)(2,1)S(1)}, bf16[128,1792]{1,0:T(8,128)(2,1)S(1)}, u32[]{:S(2)}, u32[]{:S(2)}) %collective-permute-start.19) | collective-permute-done | bytes 458784 | tf_op jit(solution)/shard_map/ppermute | solution.py:32
  185.2 2.4 %collective-permute-start.43 = (bf16[256,1792]{1,0:T(8,128)(2,1)S(1)}, bf16[256,1792]{1,0:T(8,128)(2,1)S(1)}, u32[]{:S(2)}, u32[]{:S(2)}) collective-permute-start(bf16[256,1792]{1,0:T(8,128)(2,1)S(1)} %collective-permute-done.40.refs_6_), channel_id=1, source_target_pairs={{0,24},{1,97},{8,0},{9,105},{16,8},{17,113},{24,16},{25,121},{32,5... | collective-permute-start | bytes 2752520 | tf_op jit(solution)/shard_map/ppermute | solution.py:32
  191.7 6.9 %collective-permute-done.43.refs_7_ = bf16[256,1792]{1,0:T(8,128)(2,1)S(1)} collective-permute-done((bf16[256,1792]{1,0:T(8,128)(2,1)S(1)}, bf16[256,1792]{1,0:T(8,128)(2,1)S(1)}, u32[]{:S(2)}, u32[]{:S(2)}) %collective-permute-start.43) | collective-permute-done | bytes 917536 | tf_op jit(solution)/shard_map/ppermute | solution.py:32
  199.3 5.7 %collective-permute-done.42.refs_3_ = bf16[256,1792]{1,0:T(8,128)(2,1)S(1)} collective-permute-done((bf16[256,1792]{1,0:T(8,128)(2,1)S(1)}, bf16[256,1792]{1,0:T(8,128)(2,1)S(1)}, u32[]{:S(2)}, u32[]{:S(2)}) %collective-permute-start.42) | collective-permute-done | bytes 917536 | tf_op jit(solution)/shard_map/ppermute | solution.py:32
  208.1 3.2 %collective-permute-start.50 = (bf16[128,512]{1,0:T(8,128)(2,1)S(1)}, bf16[128,512]{1,0:T(8,128)(2,1)S(1)}, u32[]{:S(2)}, u32[]{:S(2)}) collective-permute-start(bf16[128,512]{1,0:T(8,128)(2,1)S(1)} %get-tuple-element.27), channel_id=1, source_target_pairs={{0,6},{2,0},{4,2},{6,4},{1,7},{3,1},{5,3},{7,5},{8,14},{10,8},{12,... | collective-permute-start | bytes 393224 | tf_op jit(solution)/shard_map/ppermute | solution.py:24
  212.8 2.1 collective-permute-start.23
  214.9 2.3 collective-permute-start.24
  218.7 4.4 %shard_map.126 = f32[512,1792]{1,0:T(8,128)} custom-call(bf16[512,1024]{1,0:T(8,128)(2,1)S(1)} %shard_map.125.refs_0_, bf16[256,1792]{1,0:T(8,128)(2,1)S(1)} %pad_maximum_fusion.1.refs_1_, bf16[256,1792]{1,0:T(8,128)(2,1)S(1)} %collective-permute-done.17.refs_2_, bf16[128,1792]{1,0:T(8,128)(2,1)S(1)} %collective-permute-done.19.refs_3_, ...), custom_call_target="tpu_custom_call" | custom-call | tf_op jit(solution)/shard_map/pallas_call | solution.py:199
  223.1 7.1 %shard_map.124 = (f32[512,1792]{1,0:T(8,128)}, f32[512,1792]{1,0:T(8,128)}) custom-call(bf16[512,1024]{1,0:T(8,128)(2,1)S(1)} %shard_map.123.refs_0_, bf16[256,1792]{1,0:T(8,128)(2,1)S(1)} %pad_maximum_fusion.2.refs_1_, bf16[256,1792]{1,0:T(8,128)(2,1)S(1)} %collective-permute-done.39.refs_2_, bf16[256,1792]{1,0:T(8,128)(2,1)S(1)} %collective-permute-done.42.refs_3_, ...), custom_call_target="tpu_custom_call" | custom-call | tf_op jit(solution)/shard_map/pallas_call | solution.py:199
  (150 shorter events, 64.6 us)
Async XLA Ops:
  28.0 13.7 %collective-permute-start.29 = (f16[256,1792]{1,0:T(8,128)(2,1)S(1)}, f16[256,1792]{1,0:T(8,128)(2,1)S(1)}, u32[]{:S(2)}, u32[]{:S(2)}) collective-permute-start(f16[256,1792]{1,0:T(8,128)(2,1)S(1)} %fusion.12), channel_id=1, source_target_pairs={{0,24},{1,97},{8,0},{9,105},{16,8},{17,113},{24,16},{25,121},{32,5... | collective-permute-start | bytes 2752520 | tf_op jit(solution)/shard_map/ppermute | solution.py:32
  33.4 33.4 %collective-permute-start.7 = (f16[256,3584]{1,0:T(8,128)(2,1)S(1)}, f16[256,3584]{1,0:T(8,128)(2,1)S(1)}, u32[]{:S(2)}, u32[]{:S(2)}) collective-permute-start(f16[256,3584]{1,0:T(8,128)(2,1)S(1)} %fusion), channel_id=1, source_target_pairs={{0,24},{1,97},{8,0},{9,105},{16,8},{17,113},{24,16},{25,121},{32,5... | collective-permute-start | bytes 5505032 | tf_op jit(solution)/shard_map/ppermute | solution.py:32
  34.9 14.7 %collective-permute-start.30 = (f16[256,1792]{1,0:T(8,128)(2,1)S(1)}, f16[256,1792]{1,0:T(8,128)(2,1)S(1)}, u32[]{:S(2)}, u32[]{:S(2)}) collective-permute-start(f16[256,1792]{1,0:T(8,128)(2,1)S(1)} %fusion.13), channel_id=1, source_target_pairs={{0,8},{1,33},{8,16},{9,41},{16,24},{17,49},{24,0},{25,57},{32,40},... | collective-permute-start | bytes 2752520 | tf_op jit(solution)/shard_map/ppermute | solution.py:32
  42.2 24.1 %collective-permute-start.33 = (f16[128,1792]{1,0:T(8,128)(2,1)S(1)}, f16[128,1792]{1,0:T(8,128)(2,1)S(1)}, u32[]{:S(2)}, u32[]{:S(2)}) collective-permute-start(f16[128,1792]{1,0:T(8,128)(2,1)S(1)} %fusion.21), channel_id=1, source_target_pairs={{0,24},{1,97},{8,0},{9,105},{16,8},{17,113},{24,16},{25,121},{32,5... | collective-permute-start | bytes 1376264 | tf_op jit(solution)/shard_map/ppermute | solution.py:32
  47.0 35.9 %collective-permute-start.8 = (f16[256,3584]{1,0:T(8,128)(2,1)S(1)}, f16[256,3584]{1,0:T(8,128)(2,1)S(1)}, u32[]{:S(2)}, u32[]{:S(2)}) collective-permute-start(f16[256,3584]{1,0:T(8,128)(2,1)S(1)} %fusion.1), channel_id=1, source_target_pairs={{0,8},{1,33},{8,16},{9,41},{16,24},{17,49},{24,0},{25,57},{32,40},... | collective-permute-start | bytes 5505032 | tf_op jit(solution)/shard_map/ppermute | solution.py:32
  50.0 28.9 %collective-permute-start.31 = (f16[128,1792]{1,0:T(8,128)(2,1)S(1)}, f16[128,1792]{1,0:T(8,128)(2,1)S(1)}, u32[]{:S(2)}, u32[]{:S(2)}) collective-permute-start(f16[128,1792]{1,0:T(8,128)(2,1)S(1)} %fusion.20), channel_id=1, source_target_pairs={{0,8},{1,33},{8,16},{9,41},{16,24},{17,49},{24,0},{25,57},{32,40},... | collective-permute-start | bytes 1376264 | tf_op jit(solution)/shard_map/ppermute | solution.py:32
  67.5 19.6 %collective-permute-start.11 = (f16[128,3584]{1,0:T(8,128)(2,1)S(1)}, f16[128,3584]{1,0:T(8,128)(2,1)S(1)}, u32[]{:S(2)}, u32[]{:S(2)}) collective-permute-start(f16[128,3584]{1,0:T(8,128)(2,1)S(1)} %fusion.11), channel_id=1, source_target_pairs={{0,24},{1,97},{8,0},{9,105},{16,8},{17,113},{24,16},{25,121},{32,5... | collective-permute-start | bytes 2752520 | tf_op jit(solution)/shard_map/ppermute | solution.py:32
  71.3 32.9 %collective-permute-start.35 = (f16[64,1792]{1,0:T(8,128)(2,1)S(1)}, f16[64,1792]{1,0:T(8,128)(2,1)S(1)}, u32[]{:S(2)}, u32[]{:S(2)}) collective-permute-start(f16[64,1792]{1,0:T(8,128)(2,1)S(1)} %get-tuple-element.45), channel_id=1, source_target_pairs={{0,64},{1,17},{8,72},{9,25},{16,80},{17,1},{24,88},{25,9},{32,96},... | collective-permute-start | bytes 688136 | tf_op jit(solution)/shard_map/ppermute | solution.py:32
  74.8 35.4 %collective-permute-start.34 = (f16[64,1792]{1,0:T(8,128)(2,1)S(1)}, f16[64,1792]{1,0:T(8,128)(2,1)S(1)}, u32[]{:S(2)}, u32[]{:S(2)}) collective-permute-start(f16[64,1792]{1,0:T(8,128)(2,1)S(1)} %get-tuple-element.44), channel_id=1, source_target_pairs={{0,96},{1,25},{8,104},{9,1},{16,112},{17,9},{24,120},{25,17},{32,0... | collective-permute-start | bytes 688136 | tf_op jit(solution)/shard_map/ppermute | solution.py:32
  79.4 30.8 %collective-permute-start.32 = (f16[64,1792]{1,0:T(8,128)(2,1)S(1)}, f16[64,1792]{1,0:T(8,128)(2,1)S(1)}, u32[]{:S(2)}, u32[]{:S(2)}) collective-permute-start(f16[64,1792]{1,0:T(8,128)(2,1)S(1)} %slice.177), channel_id=1, source_target_pairs={{0,32},{1,9},{8,40},{9,17},{16,48},{17,25},{24,56},{25,1},{32,64},... | collective-permute-start | bytes 688136 | tf_op jit(solution)/shard_map/ppermute | solution.py:32
  83.6 19.6 %collective-permute-start.9 = (f16[128,3584]{1,0:T(8,128)(2,1)S(1)}, f16[128,3584]{1,0:T(8,128)(2,1)S(1)}, u32[]{:S(2)}, u32[]{:S(2)}) collective-permute-start(f16[128,3584]{1,0:T(8,128)(2,1)S(1)} %fusion.9), channel_id=1, source_target_pairs={{0,8},{1,33},{8,16},{9,41},{16,24},{17,49},{24,0},{25,57},{32,40},... | collective-permute-start | bytes 2752520 | tf_op jit(solution)/shard_map/ppermute | solution.py:32
  88.0 22.3 %collective-permute-start.13 = (f16[64,3584]{1,0:T(8,128)(2,1)S(1)}, f16[64,3584]{1,0:T(8,128)(2,1)S(1)}, u32[]{:S(2)}, u32[]{:S(2)}) collective-permute-start(f16[64,3584]{1,0:T(8,128)(2,1)S(1)} %get-tuple-element.37), channel_id=1, source_target_pairs={{0,64},{1,17},{8,72},{9,25},{16,80},{17,1},{24,88},{25,9},{32,96},... | collective-permute-start | bytes 1376264 | tf_op jit(solution)/shard_map/ppermute | solution.py:32
  119.3 13.8 %collective-permute-start.15 = (bf16[64,1792]{1,0:T(8,128)(2,1)S(1)}, bf16[64,1792]{1,0:T(8,128)(2,1)S(1)}, u32[]{:S(2)}, u32[]{:S(2)}) collective-permute-start(bf16[64,1792]{1,0:T(8,128)(2,1)S(1)} %get-tuple-element.34), channel_id=1, source_target_pairs={{0,64},{1,17},{8,72},{9,25},{16,80},{17,1},{24,88},{25,9},{32,96},... | collective-permute-start | bytes 688136 | tf_op jit(solution)/shard_map/ppermute | solution.py:32
  124.2 16.7 %collective-permute-start.38 = (bf16[64,3584]{1,0:T(8,128)(2,1)S(1)}, bf16[64,3584]{1,0:T(8,128)(2,1)S(1)}, u32[]{:S(2)}, u32[]{:S(2)}) collective-permute-start(bf16[64,3584]{1,0:T(8,128)(2,1)S(1)} %pad_maximum_fusion.4), channel_id=1, source_target_pairs={{0,32},{1,9},{8,40},{9,17},{16,48},{17,25},{24,56},{25,1},{32,64},... | collective-permute-start | bytes 1376264 | tf_op jit(solution)/shard_map/ppermute | solution.py:32
  124.3 28.4 %collective-permute-start.37 = (bf16[64,3584]{1,0:T(8,128)(2,1)S(1)}, bf16[64,3584]{1,0:T(8,128)(2,1)S(1)}, u32[]{:S(2)}, u32[]{:S(2)}) collective-permute-start(bf16[64,3584]{1,0:T(8,128)(2,1)S(1)} %pad_maximum_fusion.4), channel_id=1, source_target_pairs={{0,64},{1,17},{8,72},{9,25},{16,80},{17,1},{24,88},{25,9},{32,96},... | collective-permute-start | bytes 1376264 | tf_op jit(solution)/shard_map/ppermute | solution.py:32
  126.9 26.5 %collective-permute-start.36 = (bf16[64,3584]{1,0:T(8,128)(2,1)S(1)}, bf16[64,3584]{1,0:T(8,128)(2,1)S(1)}, u32[]{:S(2)}, u32[]{:S(2)}) collective-permute-start(bf16[64,3584]{1,0:T(8,128)(2,1)S(1)} %pad_maximum_fusion.4), channel_id=1, source_target_pairs={{0,96},{1,25},{8,104},{9,1},{16,112},{17,9},{24,120},{25,17},{32,0... | collective-permute-start | bytes 1376264 | tf_op jit(solution)/shard_map/ppermute | solution.py:32
  133.7 25.4 %collective-permute-start.17 = (bf16[256,1792]{1,0:T(8,128)(2,1)S(1)}, bf16[256,1792]{1,0:T(8,128)(2,1)S(1)}, u32[]{:S(2)}, u32[]{:S(2)}) collective-permute-start(bf16[256,1792]{1,0:T(8,128)(2,1)S(1)} %pad_maximum_fusion.1.refs_1_), channel_id=1, source_target_pairs={{0,24},{1,97},{8,0},{9,105},{16,8},{17,113},{24,16},{25,121},{32,5... | collective-permute-start | bytes 2752520 | tf_op jit(solution)/shard_map/ppermute | solution.py:32
  133.8 24.5 %collective-permute-start.18 = (bf16[256,1792]{1,0:T(8,128)(2,1)S(1)}, bf16[256,1792]{1,0:T(8,128)(2,1)S(1)}, u32[]{:S(2)}, u32[]{:S(2)}) collective-permute-start(bf16[256,1792]{1,0:T(8,128)(2,1)S(1)} %pad_maximum_fusion.1.refs_1_), channel_id=1, source_target_pairs={{0,8},{1,33},{8,16},{9,41},{16,24},{17,49},{24,0},{25,57},{32,40},... | collective-permute-start | bytes 2752520 | tf_op jit(solution)/shard_map/ppermute | solution.py:32
  153.4 35.6 %collective-permute-start.39 = (bf16[256,1792]{1,0:T(8,128)(2,1)S(1)}, bf16[256,1792]{1,0:T(8,128)(2,1)S(1)}, u32[]{:S(2)}, u32[]{:S(2)}) collective-permute-start(bf16[256,1792]{1,0:T(8,128)(2,1)S(1)} %pad_maximum_fusion.2.refs_1_), channel_id=1, source_target_pairs={{0,24},{1,97},{8,0},{9,105},{16,8},{17,113},{24,16},{25,121},{32,5... | collective-permute-start | bytes 2752520 | tf_op jit(solution)/shard_map/ppermute | solution.py:32
  153.5 36.3 %collective-permute-start.41 = (bf16[256,1792]{1,0:T(8,128)(2,1)S(1)}, bf16[256,1792]{1,0:T(8,128)(2,1)S(1)}, u32[]{:S(2)}, u32[]{:S(2)}) collective-permute-start(bf16[256,1792]{1,0:T(8,128)(2,1)S(1)} %pad_maximum_fusion.2.refs_1_), channel_id=1, source_target_pairs={{0,8},{1,33},{8,16},{9,41},{16,24},{17,49},{24,0},{25,57},{32,40},... | collective-permute-start | bytes 2752520 | tf_op jit(solution)/shard_map/ppermute | solution.py:32
  155.6 21.1 %collective-permute-start.40 = (bf16[256,1792]{1,0:T(8,128)(2,1)S(1)}, bf16[256,1792]{1,0:T(8,128)(2,1)S(1)}, u32[]{:S(2)}, u32[]{:S(2)}) collective-permute-start(bf16[256,1792]{1,0:T(8,128)(2,1)S(1)} %pad_maximum_fusion.3.refs_5_), channel_id=1, source_target_pairs={{0,24},{1,97},{8,0},{9,105},{16,8},{17,113},{24,16},{25,121},{32,5... | collective-permute-start | bytes 2752520 | tf_op jit(solution)/shard_map/ppermute | solution.py:32
  158.3 32.1 %collective-permute-start.44 = (bf16[256,1792]{1,0:T(8,128)(2,1)S(1)}, bf16[256,1792]{1,0:T(8,128)(2,1)S(1)}, u32[]{:S(2)}, u32[]{:S(2)}) collective-permute-start(bf16[256,1792]{1,0:T(8,128)(2,1)S(1)} %pad_maximum_fusion.3.refs_5_), channel_id=1, source_target_pairs={{0,8},{1,33},{8,16},{9,41},{16,24},{17,49},{24,0},{25,57},{32,40},... | collective-permute-start | bytes 2752520 | tf_op jit(solution)/shard_map/ppermute | solution.py:32
  159.2 23.8 %collective-permute-start.19 = (bf16[128,1792]{1,0:T(8,128)(2,1)S(1)}, bf16[128,1792]{1,0:T(8,128)(2,1)S(1)}, u32[]{:S(2)}, u32[]{:S(2)}) collective-permute-start(bf16[128,1792]{1,0:T(8,128)(2,1)S(1)} %slice.168), channel_id=1, source_target_pairs={{0,8},{1,33},{8,16},{9,41},{16,24},{17,49},{24,0},{25,57},{32,40},... | collective-permute-start | bytes 1376264 | tf_op jit(solution)/shard_map/ppermute | solution.py:32
  182.9 22.8 %collective-permute-start.45 = (f32[256,512]{1,0:T(8,128)S(1)}, f32[256,512]{1,0:T(8,128)S(1)}, u32[]{:S(2)}, u32[]{:S(2)}) collective-permute-start(f32[256,512]{1,0:T(8,128)S(1)} %convolution_add_fusion.3), channel_id=1, source_target_pairs={{0,1},{1,0},{2,3},{3,2},{4,5},{5,4},{6,7},{7,6},{8,9},{9,8},{10,11... | collective-permute-start | bytes 1572872 | tf_op jit(solution)/shard_map/ppermute | solution.py:22
  189.0 22.3 %collective-permute-start.21 = (f32[1024,512]{1,0:T(8,128)S(1)}, f32[1024,512]{1,0:T(8,128)S(1)}, u32[]{:S(2)}, u32[]{:S(2)}) collective-permute-start(f32[1024,512]{1,0:T(8,128)S(1)} %convolution_dynamic-update-slice_fusion), channel_id=1, source_target_pairs={{0,1},{1,0},{2,3},{3,2},{4,5},{5,4},{6,7},{7,6},{8,9},{9,8},{10,11... | collective-permute-start | bytes 6291464 | tf_op jit(solution)/shard_map/ppermute | solution.py:22
  189.8 16.0 %collective-permute-start.46 = (f32[256,512]{1,0:T(8,128)S(1)}, f32[256,512]{1,0:T(8,128)S(1)}, u32[]{:S(2)}, u32[]{:S(2)}) collective-permute-start(f32[256,512]{1,0:T(8,128)S(1)} %convolution_add_fusion.2), channel_id=1, source_target_pairs={{0,1},{1,0},{2,3},{3,2},{4,5},{5,4},{6,7},{7,6},{8,9},{9,8},{10,11... | collective-permute-start | bytes 1572872 | tf_op jit(solution)/shard_map/ppermute | solution.py:22
  190.4 14.6 %collective-permute-start.42 = (bf16[256,1792]{1,0:T(8,128)(2,1)S(1)}, bf16[256,1792]{1,0:T(8,128)(2,1)S(1)}, u32[]{:S(2)}, u32[]{:S(2)}) collective-permute-start(bf16[256,1792]{1,0:T(8,128)(2,1)S(1)} %collective-permute-done.41.refs_4_), channel_id=1, source_target_pairs={{0,8},{1,33},{8,16},{9,41},{16,24},{17,49},{24,0},{25,57},{32,40},... | collective-permute-start | bytes 2752520 | tf_op jit(solution)/shard_map/ppermute | solution.py:32
  208.1 22.1 %collective-permute-start.50 = (bf16[128,512]{1,0:T(8,128)(2,1)S(1)}, bf16[128,512]{1,0:T(8,128)(2,1)S(1)}, u32[]{:S(2)}, u32[]{:S(2)}) collective-permute-start(bf16[128,512]{1,0:T(8,128)(2,1)S(1)} %get-tuple-element.27), channel_id=1, source_target_pairs={{0,6},{2,0},{4,2},{6,4},{1,7},{3,1},{5,3},{7,5},{8,14},{10,8},{12,... | collective-permute-start | bytes 393224 | tf_op jit(solution)/shard_map/ppermute | solution.py:24
  211.3 18.9 %collective-permute-start.51 = (bf16[128,512]{1,0:T(8,128)(2,1)S(1)}, bf16[128,512]{1,0:T(8,128)(2,1)S(1)}, u32[]{:S(2)}, u32[]{:S(2)}) collective-permute-start(bf16[128,512]{1,0:T(8,128)(2,1)S(1)} %get-tuple-element.28), channel_id=1, source_target_pairs={{0,4},{2,6},{4,0},{6,2},{1,5},{3,7},{5,1},{7,3},{8,12},{10,14},{12... | collective-permute-start | bytes 393224 | tf_op jit(solution)/shard_map/ppermute | solution.py:24
  211.6 19.4 %collective-permute-start.22 = (bf16[128,512]{1,0:T(8,128)(2,1)S(1)}, bf16[128,512]{1,0:T(8,128)(2,1)S(1)}, u32[]{:S(2)}, u32[]{:S(2)}) collective-permute-start(bf16[128,512]{1,0:T(8,128)(2,1)S(1)} %get-tuple-element.19), channel_id=1, source_target_pairs={{0,2},{2,4},{4,6},{6,0},{1,3},{3,5},{5,7},{7,1},{8,10},{10,12},{12... | collective-permute-start | bytes 393224 | tf_op jit(solution)/shard_map/ppermute | solution.py:24
  212.8 18.2 %collective-permute-start.23 = (bf16[128,512]{1,0:T(8,128)(2,1)S(1)}, bf16[128,512]{1,0:T(8,128)(2,1)S(1)}, u32[]{:S(2)}, u32[]{:S(2)}) collective-permute-start(bf16[128,512]{1,0:T(8,128)(2,1)S(1)} %get-tuple-element.20), channel_id=1, source_target_pairs={{0,6},{2,0},{4,2},{6,4},{1,7},{3,1},{5,3},{7,5},{8,14},{10,8},{12,... | collective-permute-start | bytes 393224 | tf_op jit(solution)/shard_map/ppermute | solution.py:24
  214.9 16.1 %collective-permute-start.24 = (bf16[128,512]{1,0:T(8,128)(2,1)S(1)}, bf16[128,512]{1,0:T(8,128)(2,1)S(1)}, u32[]{:S(2)}, u32[]{:S(2)}) collective-permute-start(bf16[128,512]{1,0:T(8,128)(2,1)S(1)} %get-tuple-element.21), channel_id=1, source_target_pairs={{0,4},{2,6},{4,0},{6,2},{1,5},{3,7},{5,1},{7,3},{8,12},{10,14},{12... | collective-permute-start | bytes 393224 | tf_op jit(solution)/shard_map/ppermute | solution.py:24
  (30 other events, 208.4 us)
